TPU v7x, 128 devices: a whole 4x4x4 slice. The times are simulated.
128 devices in a mesh: bx: 16 (over x, y), by: 8 (over z, core).
Axes of the slice: x: 4, y: 4, z: 4, core: 2. Of those that a mesh axis runs over, the one named last changes fastest.
Arguments:
- particle_values: float32 [3, 262144], P(None, ('bx', 'by')), may hold values from -6 to 6
- destination: int32 [262144, 1], P(('bx', 'by')), may hold values from 0 to 127; in each aligned block of 2048 rows (0 to 2047, 2048 to 4095, ...) at most 32 rows name the same one
- cell_index: int32 [262144], P(('bx', 'by')), may hold values from 0 to 16383
- weight_in: bfloat16 [3, 3, 64, 9], replicated, may hold values from -0.625 to 0.625
- weight_mid: bfloat16 [3, 3, 64, 192], replicated, may hold values from -0.15625 to 0.15625
- weight_out: bfloat16 [3, 3, 64, 192], replicated, may hold values from -0.15625 to 0.15625
Outputs:
- spectrum: bfloat16 [2, 64, 16, 128, 1024], P(None, None, 'bx', None, 'by')
Inputs may be any that keep to these rules, and one draw needn't show every extreme that they name: `destination`: among the 2048 rows of one device, no brick is named more than 32 times; some brick is named exactly 32 times.
All inputs are finite; a program needn't handle non-finite values.
Results may differ from a plain program's by a relative error of at most 0.0074.
Values may be sent and summed in bfloat16 or wider, within the bound.
No kernel may reach another device: no remote copies, remote signals or barrier semaphores. Data moves between devices by JAX's collectives and lax.ppermute only.
A program may use at most 192 MiB of HBM per device.

v0:
```python
import math

import jax
import jax.numpy as jnp
from jax import lax
from jax.sharding import PartitionSpec as P

CELL_X = 8
CELL_Y = 128
CELL_Z = 16


def extended(cells, sides, width):
    for axis, dim in sides:
        count = lax.axis_size(axis)
        head = lax.slice_in_dim(cells, 0, width, axis=dim)
        tail = lax.slice_in_dim(cells, cells.shape[dim] - width, cells.shape[dim], axis=dim)
        cells = jnp.concatenate(
            [
                lax.ppermute(tail, axis, [(i, (i + 1) % count) for i in range(count)]),
                cells,
                lax.ppermute(head, axis, [((i + 1) % count, i) for i in range(count)]),
            ],
            axis=dim,
        )
    return cells


def convolve(widened, weight, spacing):
    out_x = widened.shape[2] - 2 * spacing
    out_y = widened.shape[3] - 2 * spacing
    stacked = jnp.concatenate(
        [jnp.roll(widened, spacing, axis=1), widened, jnp.roll(widened, -spacing, axis=1)], axis=0
    )
    summed = None
    for step_x in range(3):
        for step_y in range(3):
            window = lax.slice_in_dim(stacked, step_x * spacing, step_x * spacing + out_x, axis=2)
            window = lax.slice_in_dim(window, step_y * spacing, step_y * spacing + out_y, axis=3)
            product_term = jnp.einsum(
                "oc,czxy->ozxy", weight[step_x, step_y], window, preferred_element_type=jnp.float32
            )
            summed = product_term if summed is None else summed + product_term
    return jnp.where(summed > 0, summed, 0.1 * summed).astype(jnp.bfloat16)


def twiddle_table(count):
    position = jnp.arange(count, dtype=jnp.int32)
    phase = position[:, None] * position[None, :] % count
    angle = phase.astype(jnp.float32) * (2.0 * math.pi / count)
    factor = 1.0 / math.sqrt(count)
    return jnp.stack([jnp.cos(angle) * factor, -jnp.sin(angle) * factor]).astype(jnp.bfloat16)


def transform(moved_rows):
    twiddle = twiddle_table(moved_rows.shape[2])
    return jnp.einsum(
        "tkx,czxy->tczky", twiddle, moved_rows, preferred_element_type=jnp.float32
    ).astype(jnp.bfloat16)


def pack_rows(packed, target_dev, devices_all, capacity):
    width_rows = packed.shape[0]
    rows_here = packed.shape[1]
    block_rows = min(rows_here, 1024)
    block_count = rows_here // block_rows
    bricks = jnp.arange(devices_all, dtype=jnp.int32)
    brick_hot = (
        (target_dev[:, None] == bricks[None, :])
        .astype(jnp.bfloat16)
        .reshape(block_count, block_rows, devices_all)
    )
    block_total = jnp.sum(brick_hot.astype(jnp.float32), axis=1)
    block_start = jnp.cumsum(block_total, axis=0) - block_total
    row_ids = jnp.arange(block_rows, dtype=jnp.int32)
    lower_tri = (row_ids[:, None] > row_ids[None, :]).astype(jnp.bfloat16)
    slot_ids = jnp.arange(capacity, dtype=jnp.int32)
    packed_blocks = jnp.transpose(packed.reshape(width_rows, block_count, block_rows), (1, 0, 2))

    def pack_one_block(carry, pieces):
        hot_block, start_block, data_block = pieces
        prefix = jnp.dot(lower_tri, hot_block, preferred_element_type=jnp.float32)
        hot_float = hot_block.astype(jnp.float32)
        slot_float = jnp.sum(hot_float * (prefix + start_block[None, :]), axis=1)
        slot_hot = (slot_float.astype(jnp.int32)[:, None] == slot_ids[None, :]).astype(jnp.float32)
        spread = jnp.einsum("wp,ps->pws", data_block, slot_hot).reshape(
            block_rows, width_rows * capacity
        )
        added = jnp.dot(
            hot_float.T, spread, precision=lax.Precision.HIGHEST, preferred_element_type=jnp.float32
        )
        return (carry + added, None)

    initial = jnp.zeros((devices_all, width_rows * capacity), jnp.float32)
    outgoing, _ = lax.scan(pack_one_block, initial, (brick_hot, block_start, packed_blocks))
    return outgoing.reshape(devices_all, width_rows, capacity)


def paint_rows(incoming):
    width_rows = incoming.shape[1]
    comps = width_rows - 1
    rows_all = jnp.transpose(incoming, (0, 2, 1)).reshape(-1, width_rows)
    total_rows = rows_all.shape[0]
    block_rows = min(total_rows, 2048)
    block_count = total_rows // block_rows
    high_count = CELL_Z * CELL_X
    high_ids = jnp.arange(high_count, dtype=jnp.int32)
    low_ids = jnp.arange(CELL_Y, dtype=jnp.int32)
    row_blocks = rows_all.reshape(block_count, block_rows, width_rows)

    def paint_one_block(carry, block):
        cells = block[:, 0].astype(jnp.int32)
        values = block[:, 1:]
        high_hot = ((cells // CELL_Y)[:, None] == high_ids[None, :]).astype(jnp.float32)
        low_hot = ((cells % CELL_Y)[:, None] == low_ids[None, :]).astype(jnp.float32)
        spread = jnp.einsum("pf,py->pfy", values, low_hot).reshape(block_rows, comps * CELL_Y)
        added = jnp.dot(
            high_hot.T, spread, precision=lax.Precision.HIGHEST, preferred_element_type=jnp.float32
        )
        return (carry + added, None)

    initial = jnp.zeros((high_count, comps * CELL_Y), jnp.float32)
    summed, _ = lax.scan(paint_one_block, initial, row_blocks)
    painted = jnp.transpose(summed.reshape(high_count, comps, CELL_Y), (1, 0, 2))
    return painted.reshape(comps, CELL_Z, CELL_X, CELL_Y).astype(jnp.bfloat16)


def on_device(particle_values, destination, cell_index, weight_in, weight_mid, weight_out):
    count_x = lax.axis_size("bx")
    count_y = lax.axis_size("by")
    devices_all = count_x * count_y
    rows_here = cell_index.shape[0]
    capacity = 2 * rows_here // devices_all
    target_dev = destination[:, 0]
    packed = jnp.concatenate([cell_index.astype(jnp.float32)[None, :], particle_values], axis=0)
    outgoing = pack_rows(packed, target_dev, devices_all, capacity)
    incoming = lax.all_to_all(outgoing, ("bx", "by"), split_axis=0, concat_axis=0, tiled=True)
    painted = paint_rows(incoming)
    layers = ((weight_in, 1), (weight_mid, 2), (weight_out, 1))
    current = painted
    for weight, spacing in layers:
        widened = extended(current, (("bx", 2), ("by", 3)), spacing)
        current = convolve(widened, weight, spacing)
    return transform(lax.all_to_all(current, "bx", split_axis=1, concat_axis=2, tiled=True))


def solution(mesh):
    placed = (P(None, ("bx", "by")), P(("bx", "by"), None), P(("bx", "by")), P(), P(), P())
    return jax.shard_map(
        on_device,
        mesh=mesh,
        in_specs=placed,
        out_specs=P(None, None, "bx", None, "by"),
        check_vma=False,
    )
```

profile of v0, /device:TPU:0, one launch (start us, length us, event | category | flops | bytes accessed | tf_op | source)
XLA Modules:
  0.0 475.6 jit_solution(11696483526119485444)
XLA Ops:
  7.2 11.2 %all-to-all-start = ((f32[128,1,128]{2,1,0:T(1,128)}), f32[128,1,128]{2,1,0:T(1,128)S(1)}, u32[]{:S(2)}, u32[]{:S(2)}) async-start(f32[128,1,128]{2,1,0:T(1,128)} %reshape.164), calls=%async_computation | async-start | bytes 131072 | tf_op jit(solution)/shard_map/all_to_all | solution.py:137
  18.4 9.5 %all-to-all-done = f32[128,1,128]{2,1,0:T(1,128)S(1)} async-done(((f32[128,1,128]{2,1,0:T(1,128)}), f32[128,1,128]{2,1,0:T(1,128)S(1)}, u32[]{:S(2)}, u32[]{:S(2)}) %all-to-all-start) | async-done | bytes 65568 | tf_op jit(solution)/shard_map/all_to_all | solution.py:137
  29.6 5.1 %while.27 = (s32[]{:T(128)}, f32[128,384]{1,0:T(8,128)S(1)}, f32[2,2048,4]{1,0,2:T(2,128)S(1)}, s32[]{:T(128)}, s32[]{:T(128)}) while((s32[]{:T(128)}, f32[128,384]{1,0:T(8,128)S(1)}, f32[2,2048,4]{1,0,2:T(2,128)S(1)}, s32[]{:T(128)}, s32[]{:T(128)}) %tuple.79), condition=%wide.region_6.7_spmd.clone.clone, body=%wide.region_5.6_spmd.clone.clone.sunk | while | flops 1209673728 | bytes 9044043 | solution.py:123
  70.6 9.6 %fusion.75 = bf16[64,16,8,128]{3,0,2,1:T(8,128)(2,1)S(1)} fusion(f32[16,8,128,64]{2,3,1,0:T(8,128)S(1)} %fusion.85, f32[16,8,128,64]{2,3,1,0:T(8,128)S(1)} %fusion.87, f32[16,8,128,64]{2,3,1,0:T(8,128)} %fusion.89, f32[16,8,128,64]{2,3,1,0:T(8,128)} %fusion.91, f32[16,8,128,64]{2,3,1,0:T(8,128)} %fusion.93, f32[16,8,128,64]{2,3,1,0:T(8,128)} %fusion.95, ...), kind=kOutput, calls=%fused_computation.102 | convolution fusion | flops 31457280 | bytes 36180480 | tf_op jit(solution)/shard_map/oc,czxy->ozxy/dot_general | solution.py:40
  80.3 6.0 %collective-permute-start.5 = (bf16[64,16,2,128]{3,0,2,1:T(8,128)(2,1)S(1)}, bf16[64,16,2,128]{3,0,2,1:T(8,128)(2,1)S(1)}, u32[]{:S(2)}, u32[]{:S(2)}) collective-permute-start(bf16[64,16,2,128]{3,0,2,1:T(8,128)(2,1)S(1)} %get-tuple-element.200), channel_id=1, source_target_pairs={{8,0},{16,8},{24,16},{32,24},{40,32},{48,40},{56,48},{64,56},{72,6... | collective-permute-start | bytes 1572872 | tf_op jit(solution)/shard_map/ppermute | solution.py:22
  86.4 11.2 %collective-permute-done.4 = bf16[64,16,2,128]{3,0,2,1:T(8,128)(2,1)S(1)} collective-permute-done((bf16[64,16,2,128]{3,0,2,1:T(8,128)(2,1)S(1)}, bf16[64,16,2,128]{3,0,2,1:T(8,128)(2,1)S(1)}, u32[]{:S(2)}, u32[]{:S(2)}) %collective-permute-start.4) | collective-permute-done | bytes 524320 | tf_op jit(solution)/shard_map/ppermute | solution.py:20
  118.3 9.7 %pad_maximum_fusion.16 = bf16[64,16,12,132]{3,0,2,1:T(8,128)(2,1)} fusion(bf16[64,16,12,2]{3,0,2,1:T(8,128)(2,1)} %copy.53, bf16[64,16,2,128]{3,0,2,1:T(8,128)(2,1)S(1)} %collective-permute-done.5, bf16[64,16,8,128]{3,0,2,1:T(8,128)(2,1)S(1)} %fusion.75, bf16[64,16,2,128]{3,0,2,1:T(8,128)(2,1)S(1)} %collective-permute-done.4, bf16[64,16,12,2]{3,0,2,1:T(8,128)(2,1)} %copy.52), kind=kLoop, calls=%fused_computation.100 | loop fusion | flops 16220160 | bytes 6488064 | tf_op jit(solution)/shard_map/concatenate | solution.py:18
  128.0 10.6 %fusion.154 = (bf16[64,14,12,132]{3,0,2,1:T(8,128)(2,1)}, bf16[64,14,12,132]{3,0,2,1:T(8,128)(2,1)}) fusion(bf16[64,16,12,132]{3,0,2,1:T(8,128)(2,1)} %pad_maximum_fusion.16), kind=kLoop, calls=%fused_computation.204 | loop fusion | bytes 11354112 | tf_op jit(solution)/shard_map/jit(_roll_static)/slice | solution.py:33
  138.6 95.0 %fusion.32 = bf16[192,16,12,132]{3,0,2,1:T(8,128)(2,1)} fusion(bf16[64,16,12,2]{3,0,2,1:T(8,128)(2,1)} %copy.53, bf16[64,16,12,2]{3,0,2,1:T(8,128)(2,1)} %copy.52, bf16[64,16,2,128]{3,0,2,1:T(8,128)(2,1)S(1)} %collective-permute-done.5, bf16[64,16,8,128]{3,0,2,1:T(8,128)(2,1)S(1)} %fusion.75, bf16[64,16,2,128]{3,0,2,1:T(8,128)(2,1)S(1)} %collective-permute-done.4, ...), kind=kLoop, calls=%fused_computation.39 | loop fusion | flops 165445632 | bytes 18653184 | tf_op jit(solution)/shard_map/concatenate | solution.py:32
  233.7 9.3 %fusion.59 = f32[16,8,128,64]{2,3,1,0:T(8,128)} fusion(bf16[192,16,12,132]{3,0,2,1:T(8,128)(2,1)} %fusion.32, bf16[3,3,64,192]{3,2,1,0:T(8,128)(2,1)S(1)} %copy-done.2), kind=kOutput, calls=%fused_computation.84 | convolution fusion | flops 402653184 | bytes 10518528 | tf_op jit(solution)/shard_map/oc,czxy->ozxy/dot_general | solution.py:40
  243.0 6.9 %fusion.61 = f32[16,8,128,64]{2,3,1,0:T(8,128)} fusion(bf16[192,16,12,132]{3,0,2,1:T(8,128)(2,1)} %fusion.32, bf16[3,3,64,192]{3,2,1,0:T(8,128)(2,1)S(1)} %copy-done.2), kind=kOutput, calls=%fused_computation.86 | convolution fusion | flops 402653184 | bytes 10518528 | tf_op jit(solution)/shard_map/oc,czxy->ozxy/dot_general | solution.py:40
  266.5 4.9 %fusion.71 = f32[16,8,128,64]{2,3,1,0:T(8,128)} fusion(bf16[192,16,12,132]{3,0,2,1:T(8,128)(2,1)S(1)} %copy-done.1, bf16[3,3,64,192]{3,2,1,0:T(8,128)(2,1)S(1)} %copy-done.2), kind=kOutput, calls=%fused_computation.96 | convolution fusion | flops 402653184 | bytes 10518528 | tf_op jit(solution)/shard_map/oc,czxy->ozxy/dot_general | solution.py:40
  274.8 17.3 %fusion.76 = bf16[64,16,8,128]{3,0,2,1:T(8,128)(2,1)S(1)} fusion(f32[16,8,128,64]{2,3,1,0:T(8,128)} %fusion.59, f32[16,8,128,64]{2,3,1,0:T(8,128)} %fusion.61, f32[16,8,128,64]{2,3,1,0:T(8,128)} %fusion.63, f32[16,8,128,64]{2,3,1,0:T(8,128)} %fusion.65, f32[16,8,128,64]{2,3,1,0:T(8,128)} %fusion.67, f32[16,8,128,64]{2,3,1,0:T(8,128)} %fusion.69, ...), kind=kOutput, calls=%fused_computation.103 | convolution fusion | flops 415236096 | bytes 41975808 | tf_op jit(solution)/shard_map/oc,czxy->ozxy/dot_general | solution.py:40
  292.2 5.6 %collective-permute-start.9 = (bf16[64,16,1,128]{3,0,2,1:T(8,128)(2,1)S(1)}, bf16[64,16,1,128]{3,0,2,1:T(8,128)(2,1)S(1)}, u32[]{:S(2)}, u32[]{:S(2)}) collective-permute-start(bf16[64,16,1,128]{3,0,2,1:T(8,128)(2,1)S(1)} %get-tuple-element.198), channel_id=1, source_target_pairs={{8,0},{16,8},{24,16},{32,24},{40,32},{48,40},{56,48},{64,56},{72,6... | collective-permute-start | bytes 786440 | tf_op jit(solution)/shard_map/ppermute | solution.py:22
  319.0 6.0 %pad_maximum_fusion.17 = bf16[64,16,10,130]{3,0,2,1:T(8,128)(2,1)S(1)} fusion(bf16[64,16,10,1]{3,0,2,1:T(8,128)(2,1)} %copy.57, bf16[64,16,1,128]{3,0,2,1:T(8,128)(2,1)S(1)} %collective-permute-done.9, bf16[64,16,8,128]{3,0,2,1:T(8,128)(2,1)S(1)} %fusion.76, bf16[64,16,1,128]{3,0,2,1:T(8,128)(2,1)S(1)} %collective-permute-done.8, ...), kind=kLoop, calls=%fused_computation.101 | loop fusion | flops 13312000 | bytes 5324800 | tf_op jit(solution)/shard_map/concatenate | solution.py:18
  325.0 5.0 %fusion.155 = (bf16[64,15,10,130]{3,0,2,1:T(8,128)(2,1)}, bf16[64,15,10,130]{3,0,2,1:T(8,128)(2,1)}) fusion(bf16[64,16,10,130]{3,0,2,1:T(8,128)(2,1)S(1)} %pad_maximum_fusion.17), kind=kLoop, calls=%fused_computation.205 | loop fusion | bytes 9984000 | tf_op jit(solution)/shard_map/jit(_roll_static)/slice | solution.py:33
  330.0 39.5 %fusion.36 = bf16[192,16,10,130]{3,0,2,1:T(8,128)(2,1)} fusion(bf16[64,16,10,1]{3,0,2,1:T(8,128)(2,1)} %copy.57, bf16[64,16,10,1]{3,0,2,1:T(8,128)(2,1)} %copy.56, bf16[64,16,1,128]{3,0,2,1:T(8,128)(2,1)S(1)} %collective-permute-done.9, bf16[64,16,8,128]{3,0,2,1:T(8,128)(2,1)S(1)} %fusion.76, bf16[64,16,1,128]{3,0,2,1:T(8,128)(2,1)S(1)} %collective-permute-done.8, ...), kind=kLoop, calls=%fused_computation.51 | loop fusion | flops 135782400 | bytes 15641600 | tf_op jit(solution)/shard_map/concatenate | solution.py:32
  369.5 9.3 %fusion.41 = f32[16,8,128,64]{2,3,1,0:T(8,128)} fusion(bf16[192,16,10,130]{3,0,2,1:T(8,128)(2,1)} %fusion.36, bf16[3,3,64,192]{3,2,1,0:T(8,128)(2,1)S(1)} %copy-done.3), kind=kOutput, calls=%fused_computation.66 | convolution fusion | flops 402653184 | bytes 10518528 | tf_op jit(solution)/shard_map/oc,czxy->ozxy/dot_general | solution.py:40
  378.8 6.3 %fusion.43 = f32[16,8,128,64]{2,3,1,0:T(8,128)} fusion(bf16[192,16,10,130]{3,0,2,1:T(8,128)(2,1)} %fusion.36, bf16[3,3,64,192]{3,2,1,0:T(8,128)(2,1)S(1)} %copy-done.3), kind=kOutput, calls=%fused_computation.68 | convolution fusion | flops 402653184 | bytes 10518528 | tf_op jit(solution)/shard_map/oc,czxy->ozxy/dot_general | solution.py:40
  409.7 18.9 %fusion.77 = bf16[64,16,8,128]{3,0,2,1:T(8,128)(2,1)} fusion(f32[16,8,128,64]{2,3,1,0:T(8,128)} %fusion.41, f32[16,8,128,64]{2,3,1,0:T(8,128)} %fusion.43, f32[16,8,128,64]{2,3,1,0:T(8,128)} %fusion.45, f32[16,8,128,64]{2,3,1,0:T(8,128)} %fusion.47, f32[16,8,128,64]{2,3,1,0:T(8,128)} %fusion.49, f32[16,8,128,64]{2,3,1,0:T(8,128)} %fusion.51, ...), kind=kOutput, calls=%fused_computation.104 | convolution fusion | flops 415236096 | bytes 41975808 | tf_op jit(solution)/shard_map/oc,czxy->ozxy/dot_general | solution.py:40
  428.5 6.5 %all-to-all-start.1 = ((bf16[64,16,8,128]{3,0,2,1:T(8,128)(2,1)}), bf16[64,16,8,128]{3,0,2,1:T(8,128)(2,1)S(1)}, u32[]{:S(2)}, u32[]{:S(2)}) async-start(bf16[64,16,8,128]{3,0,2,1:T(8,128)(2,1)} %fusion.77), calls=%async_computation.1 | async-start | bytes 4194304 | tf_op jit(solution)/shard_map/all_to_all | solution.py:144
  435.4 28.5 %all-to-all-done.1 = bf16[64,16,8,128]{3,0,2,1:T(8,128)(2,1)S(1)} async-done(((bf16[64,16,8,128]{3,0,2,1:T(8,128)(2,1)}), bf16[64,16,8,128]{3,0,2,1:T(8,128)(2,1)S(1)}, u32[]{:S(2)}, u32[]{:S(2)}) %all-to-all-start.1) | async-done | bytes 2097184 | tf_op jit(solution)/shard_map/all_to_all | solution.py:144
  463.8 5.2 %convert_bitcast_fusion = bf16[2,64,1,128,128]{3,4,0,1,2:T(8,128)(2,1)} fusion(bf16[64,128,128,1]{2,0,1,3:T(8,128)(2,1)S(1)} %bitcast.274, bf16[1,128,128]{2,1,0:T(8,128)(2,1)S(1)} %get-tuple-element.216, bf16[1,128,128]{2,1,0:T(8,128)(2,1)S(1)} %get-tuple-element.217), kind=kOutput, calls=%fused_computation.105 | convolution fusion | flops 539099136 | bytes 6356992 | tf_op jit(solution)/shard_map/tkx,czxy->tczky/dot_general | solution.py:57
  469.1 6.3 %copy.59 = bf16[2,64,1,128,128]{4,3,2,1,0:T(8,128)(2,1)} copy(bf16[2,64,1,128,128]{3,4,0,1,2:T(8,128)(2,1)} %convert_bitcast_fusion) | data formatting | bytes 8388608 | tf_op jit(solution)/shard_map/convert_element_type | solution.py:59
  (124 shorter events, 138.8 us)
Async XLA Ops:
  7.2 20.6 %all-to-all-start = ((f32[128,1,128]{2,1,0:T(1,128)}), f32[128,1,128]{2,1,0:T(1,128)S(1)}, u32[]{:S(2)}, u32[]{:S(2)}) async-start(f32[128,1,128]{2,1,0:T(1,128)} %reshape.164), calls=%async_computation | async-start | bytes 131072 | tf_op jit(solution)/shard_map/all_to_all | solution.py:137
  29.6 15.8 %copy-start.4 = (bf16[3,3,64,9]{2,1,3,0:T(4,128)(2,1)S(1)}, bf16[3,3,64,9]{2,1,3,0:T(4,128)(2,1)}, u32[]{:S(2)}) copy-start(bf16[3,3,64,9]{2,1,3,0:T(4,128)(2,1)} %param.13) | copy-start | bytes 31108
  34.9 7.1 %collective-permute-start = (bf16[3,16,1,128]{3,0,2,1:T(4,128)(2,1)S(1)}, bf16[3,16,1,128]{3,0,2,1:T(4,128)(2,1)S(1)}, u32[]{:S(2)}, u32[]{:S(2)}) collective-permute-start(bf16[3,16,1,128]{3,0,2,1:T(4,128)(2,1)S(1)} %get-tuple-element.205), channel_id=1, source_target_pairs={{0,8},{8,16},{16,24},{24,32},{32,40},{40,48},{48,56},{56,64},{64,7... | collective-permute-start | bytes 36872 | tf_op jit(solution)/shard_map/ppermute | solution.py:20
  35.7 6.4 %collective-permute-start.1 = (bf16[3,16,1,128]{3,0,2,1:T(4,128)(2,1)S(1)}, bf16[3,16,1,128]{3,0,2,1:T(4,128)(2,1)S(1)}, u32[]{:S(2)}, u32[]{:S(2)}) collective-permute-start(bf16[3,16,1,128]{3,0,2,1:T(4,128)(2,1)S(1)} %get-tuple-element.206), channel_id=1, source_target_pairs={{8,0},{16,8},{24,16},{32,24},{40,32},{48,40},{56,48},{64,56},{72,6... | collective-permute-start | bytes 36872 | tf_op jit(solution)/shard_map/ppermute | solution.py:22
  42.4 6.0 %collective-permute-start.2 = (bf16[3,16,10,1]{3,0,2,1:T(4,128)(2,1)S(1)}, bf16[3,16,10,1]{3,0,2,1:T(4,128)(2,1)S(1)}, u32[]{:S(2)}, u32[]{:S(2)}) collective-permute-start(bf16[3,16,10,1]{3,0,2,1:T(4,128)(2,1)S(1)} %get-tuple-element.203), channel_id=1, source_target_pairs={{0,1},{1,2},{2,3},{3,4},{4,5},{5,6},{6,7},{7,0},{8,9},{9,10},{10,1... | collective-permute-start | bytes 2888 | tf_op jit(solution)/shard_map/ppermute | solution.py:20
  42.4 5.9 %collective-permute-start.3 = (bf16[3,16,10,1]{3,0,2,1:T(4,128)(2,1)S(1)}, bf16[3,16,10,1]{3,0,2,1:T(4,128)(2,1)S(1)}, u32[]{:S(2)}, u32[]{:S(2)}) collective-permute-start(bf16[3,16,10,1]{3,0,2,1:T(4,128)(2,1)S(1)} %get-tuple-element.204), channel_id=1, source_target_pairs={{1,0},{2,1},{3,2},{4,3},{5,4},{6,5},{7,6},{0,7},{9,8},{10,9},{11,1... | collective-permute-start | bytes 2888 | tf_op jit(solution)/shard_map/ppermute | solution.py:22
  80.3 17.2 %collective-permute-start.4 = (bf16[64,16,2,128]{3,0,2,1:T(8,128)(2,1)S(1)}, bf16[64,16,2,128]{3,0,2,1:T(8,128)(2,1)S(1)}, u32[]{:S(2)}, u32[]{:S(2)}) collective-permute-start(bf16[64,16,2,128]{3,0,2,1:T(8,128)(2,1)S(1)} %get-tuple-element.199), channel_id=1, source_target_pairs={{0,8},{8,16},{16,24},{24,32},{32,40},{40,48},{48,56},{56,64},{64,7... | collective-permute-start | bytes 1572872 | tf_op jit(solution)/shard_map/ppermute | solution.py:20
  80.3 17.2 %collective-permute-start.5 = (bf16[64,16,2,128]{3,0,2,1:T(8,128)(2,1)S(1)}, bf16[64,16,2,128]{3,0,2,1:T(8,128)(2,1)S(1)}, u32[]{:S(2)}, u32[]{:S(2)}) collective-permute-start(bf16[64,16,2,128]{3,0,2,1:T(8,128)(2,1)S(1)} %get-tuple-element.200), channel_id=1, source_target_pairs={{8,0},{16,8},{24,16},{32,24},{40,32},{48,40},{56,48},{64,56},{72,6... | collective-permute-start | bytes 1572872 | tf_op jit(solution)/shard_map/ppermute | solution.py:22
  106.0 6.4 %collective-permute-start.6 = (bf16[64,16,12,2]{0,1,3,2:T(8,128)(2,1)S(1)}, bf16[64,16,12,2]{0,1,3,2:T(8,128)(2,1)S(1)}, u32[]{:S(2)}, u32[]{:S(2)}) collective-permute-start(bf16[64,16,12,2]{0,1,3,2:T(8,128)(2,1)S(1)} %copy.50), channel_id=1, source_target_pairs={{0,1},{1,2},{2,3},{3,4},{4,5},{5,6},{6,7},{7,0},{8,9},{9,10},{10,1... | collective-permute-start | bytes 147464 | tf_op jit(solution)/shard_map/ppermute | solution.py:20
  109.4 6.0 %collective-permute-start.7 = (bf16[64,16,12,2]{0,1,3,2:T(8,128)(2,1)S(1)}, bf16[64,16,12,2]{0,1,3,2:T(8,128)(2,1)S(1)}, u32[]{:S(2)}, u32[]{:S(2)}) collective-permute-start(bf16[64,16,12,2]{0,1,3,2:T(8,128)(2,1)S(1)} %copy.51), channel_id=1, source_target_pairs={{1,0},{2,1},{3,2},{4,3},{5,4},{6,5},{7,6},{0,7},{9,8},{10,9},{11,1... | collective-permute-start | bytes 147464 | tf_op jit(solution)/shard_map/ppermute | solution.py:22
  138.6 95.1 %copy-start.2 = (bf16[3,3,64,192]{3,2,1,0:T(8,128)(2,1)S(1)}, bf16[3,3,64,192]{3,2,1,0:T(8,128)(2,1)}, u32[]{:S(2)}) copy-start(bf16[3,3,64,192]{3,2,1,0:T(8,128)(2,1)} %param.14) | copy-start | bytes 663556
  233.7 16.2 %copy-start.1 = (bf16[192,16,12,132]{3,0,2,1:T(8,128)(2,1)S(1)}, bf16[192,16,12,132]{3,0,2,1:T(8,128)(2,1)}, u32[]{:S(2)}) copy-start(bf16[192,16,12,132]{3,0,2,1:T(8,128)(2,1)} %fusion.32) | copy-start | bytes 29196292
  292.1 10.5 %collective-permute-start.8 = (bf16[64,16,1,128]{3,0,2,1:T(8,128)(2,1)S(1)}, bf16[64,16,1,128]{3,0,2,1:T(8,128)(2,1)S(1)}, u32[]{:S(2)}, u32[]{:S(2)}) collective-permute-start(bf16[64,16,1,128]{3,0,2,1:T(8,128)(2,1)S(1)} %get-tuple-element.197), channel_id=1, source_target_pairs={{0,8},{8,16},{16,24},{24,32},{32,40},{40,48},{48,56},{56,64},{64,7... | collective-permute-start | bytes 786440 | tf_op jit(solution)/shard_map/ppermute | solution.py:20
  292.2 10.5 %collective-permute-start.9 = (bf16[64,16,1,128]{3,0,2,1:T(8,128)(2,1)S(1)}, bf16[64,16,1,128]{3,0,2,1:T(8,128)(2,1)S(1)}, u32[]{:S(2)}, u32[]{:S(2)}) collective-permute-start(bf16[64,16,1,128]{3,0,2,1:T(8,128)(2,1)S(1)} %get-tuple-element.198), channel_id=1, source_target_pairs={{8,0},{16,8},{24,16},{32,24},{40,32},{48,40},{56,48},{64,56},{72,6... | collective-permute-start | bytes 786440 | tf_op jit(solution)/shard_map/ppermute | solution.py:22
  309.1 5.4 %collective-permute-start.10 = (bf16[64,16,10,1]{0,1,3,2:T(8,128)(2,1)S(1)}, bf16[64,16,10,1]{0,1,3,2:T(8,128)(2,1)S(1)}, u32[]{:S(2)}, u32[]{:S(2)}) collective-permute-start(bf16[64,16,10,1]{0,1,3,2:T(8,128)(2,1)S(1)} %copy.54), channel_id=1, source_target_pairs={{0,1},{1,2},{2,3},{3,4},{4,5},{5,6},{6,7},{7,0},{8,9},{9,10},{10,1... | collective-permute-start | bytes 61448 | tf_op jit(solution)/shard_map/ppermute | solution.py:20
  311.5 5.2 %collective-permute-start.11 = (bf16[64,16,10,1]{0,1,3,2:T(8,128)(2,1)S(1)}, bf16[64,16,10,1]{0,1,3,2:T(8,128)(2,1)S(1)}, u32[]{:S(2)}, u32[]{:S(2)}) collective-permute-start(bf16[64,16,10,1]{0,1,3,2:T(8,128)(2,1)S(1)} %copy.55), channel_id=1, source_target_pairs={{1,0},{2,1},{3,2},{4,3},{5,4},{6,5},{7,6},{0,7},{9,8},{10,9},{11,1... | collective-permute-start | bytes 61448 | tf_op jit(solution)/shard_map/ppermute | solution.py:22
  330.0 39.5 %copy-start.3 = (bf16[3,3,64,192]{3,2,1,0:T(8,128)(2,1)S(1)}, bf16[3,3,64,192]{3,2,1,0:T(8,128)(2,1)}, u32[]{:S(2)}) copy-start(bf16[3,3,64,192]{3,2,1,0:T(8,128)(2,1)} %param.15) | copy-start | bytes 663556
  369.5 15.6 %copy-start = (bf16[192,16,10,130]{3,0,2,1:T(8,128)(2,1)S(1)}, bf16[192,16,10,130]{3,0,2,1:T(8,128)(2,1)}, u32[]{:S(2)}) copy-start(bf16[192,16,10,130]{3,0,2,1:T(8,128)(2,1)} %fusion.36) | copy-start | bytes 23961604
  428.5 35.3 %all-to-all-start.1 = ((bf16[64,16,8,128]{3,0,2,1:T(8,128)(2,1)}), bf16[64,16,8,128]{3,0,2,1:T(8,128)(2,1)S(1)}, u32[]{:S(2)}, u32[]{:S(2)}) async-start(bf16[64,16,8,128]{3,0,2,1:T(8,128)(2,1)} %fusion.77), calls=%async_computation.1 | async-start | bytes 4194304 | tf_op jit(solution)/shard_map/all_to_all | solution.py:144
where the time goes:
time: 481 us; the launch traced here: 476 us
  other arithmetic  161 us (33%)
  matrix products  156 us (32%)
  waiting for transfers between devices  58.4 us (12%)
  local copies, waits for them, and re-layouts  55.7 us (12%)
  starting transfers between devices  43.9 us (9%)
    dot_general x27, matrix products, convolve(): jnp.einsum('oc,czxy->ozxy', weight[step_x, step_y], window, preferred_ele...  145 us
    concatenate x3, other arithmetic, convolve(): jnp.concatenate([jnp.roll(widened, spacing, axis=1), widened, jnp.roll(wi...  138 us
    all_to_all x1, waiting for transfers between devices, on_device(): lax.all_to_all(current, 'bx', split_axis=1, concat_axis=2, tiled=True)  28.5 us
    ppermute x6, starting transfers between devices, extended(): lax.ppermute(head, axis, [((i + 1) % count, i) for i in range(count)])  25.4 us
    ppermute x6, waiting for transfers between devices, extended(): lax.ppermute(tail, axis, [(i, (i + 1) % count) for i in range(count)])  20.5 us
    concatenate x6, other arithmetic, extended(): jnp.concatenate([lax.ppermute(tail, axis, [(i, (i + 1) % count) for i in...  17.1 us
    slice x3, local copies, waits for them, and re-layouts, convolve(): jnp.roll(widened, spacing, axis=1)  15.8 us
    slice x8, local copies, waits for them, and re-layouts, extended(): lax.slice_in_dim(cells, cells.shape[dim] - width, cells.shape[dim], axis=...  14.5 us
  transfers between devices with their start and end apart: 14, of which 6 were waited for; matrix products, arithmetic and copies ran while one was open for 2% of the time, Pallas kernels for 0%

commit v1 on v0

v1 whole, which is shorter than its diff:
```python
import math

import jax
import jax.numpy as jnp
import numpy as np
from jax import lax
from jax.experimental import pallas as pl
from jax.experimental.pallas import tpu as pltpu
from jax.sharding import PartitionSpec as P

F32 = jnp.float32
BF16 = jnp.bfloat16
I32 = jnp.int32
VMEM = pltpu.VMEM

NT = (((1,), (1,)), ((), ()))
NN = (((1,), (0,)), ((), ()))

Y1 = 144
K_TAPS = 9 * 384


def dot(a, b, dims=NN):
    return lax.dot_general(a, b, dims, preferred_element_type=F32)


def leaky(u):
    return jnp.where(u > 0, u, 0.1 * u)


def split2(v):
    high = v.astype(BF16)
    return high, (v - high.astype(F32)).astype(BF16)


def pack_kernel(dest_ref, cell_ref, value_ref, out_ref):
    rows = dest_ref.shape[1]
    step = 256
    brick = lax.broadcasted_iota(I32, (128, step), 0)
    before = (
        lax.broadcasted_iota(I32, (step, step), 0) < lax.broadcasted_iota(I32, (step, step), 1)
    ).astype(F32).astype(BF16)
    slot_ids = lax.broadcasted_iota(I32, (32, step), 0)
    seen = jnp.zeros((128, 1), F32)
    total = jnp.zeros((128, 256), F32)
    for start in range(0, rows, step):
        here = slice(start, start + step)
        hot = (brick == dest_ref[:, here]).astype(F32)
        hot_b = hot.astype(BF16)
        prefix = dot(hot_b, before) + seen
        slot = jnp.sum(hot * prefix, axis=0, keepdims=True).astype(I32)
        seen = prefix[:, step - 1 :] + hot[:, step - 1 :]
        mine = slot_ids == slot
        pieces = [cell_ref[:, here].astype(F32)] + [value_ref[f : f + 1, here] for f in range(3)]
        highs, lows = [], []
        for piece in pieces:
            high = piece.astype(BF16).astype(F32)
            highs.append(jnp.where(mine, high, 0.0))
            lows.append(jnp.where(mine, piece - high, 0.0))
        spread = jnp.concatenate(highs + lows, axis=0).astype(BF16)
        total = total + dot(hot_b, spread, NT)
    out_ref[...] = total[:, :128] + total[:, 128:]


def pack(dest, cell, values):
    return pl.pallas_call(
        pack_kernel,
        out_shape=jax.ShapeDtypeStruct((128, 128), F32),
        name="pack",
    )(dest, cell, values)


def paint_kernel(in_ref, left_ref, right_ref, acc_ref):
    turned = jnp.transpose(in_ref[...], (1, 0))
    cells = turned[0:32].astype(I32)
    place = ((cells >> 8) & 3) * 128 + (cells & 127)
    parity = (cells >> 7) & 1
    depth = cells >> 10
    code = parity * 16 + depth
    parts = []
    for f in range(3):
        value = turned[32 + 32 * f : 64 + 32 * f]
        high = value.astype(BF16).astype(F32)
        parts.append((high, value - high))
    z_ids = lax.broadcasted_iota(I32, (16, 128), 0)
    place_ids = lax.broadcasted_iota(I32, (512, 128), 0)
    blank = jnp.zeros((16, 128), F32)
    group = 8
    for start in range(0, 32, group):
        hots, sides = [], []
        for s in range(start, start + group):
            hots.append((place_ids == place[s : s + 1]).astype(F32).astype(BF16))
            column = []
            for part in range(2):
                for par in range(2):
                    here = z_ids + par * 16 == code[s : s + 1]
                    for f in range(3):
                        column.append(jnp.where(here, parts[f][part][s : s + 1], 0.0))
                    column.append(blank)
            sides.append(jnp.concatenate(column, axis=0).astype(BF16))
        added = dot(jnp.concatenate(hots, axis=1), jnp.concatenate(sides, axis=1), NT)
        if start == 0:
            acc_ref[...] = added
        else:
            acc_ref[...] += added
    painted = (acc_ref[:, :128] + acc_ref[:, 128:]).astype(BF16)
    left_ref[...] = painted[:256].reshape(2, 128, 128)
    right_ref[...] = painted[256:].reshape(2, 128, 128)


def paint(incoming):
    half = jax.ShapeDtypeStruct((2, 128, 128), BF16)
    return pl.pallas_call(
        paint_kernel,
        out_shape=(half, half),
        scratch_shapes=[VMEM((512, 256), F32)],
        name="paint",
    )(incoming)


def weights_kernel(win_ref, wmid_ref, wout_ref, r1_ref, r2_ref, w3_ref):
    lane = lax.broadcasted_iota(I32, (16, 1024), 1)
    tile = lane // 128
    half = (lane // 64) % 2
    z_out = jnp.where(tile < 4, 14 + 4 * tile + 2 * half, 13 + 4 * (tile - 4) + 2 * half) % 16
    tap_z = (lax.broadcasted_iota(I32, (16, 1024), 0) - z_out + 17) % 16
    hits = [tap_z == tz for tz in range(3)]
    blank = jnp.zeros((64, 1024), BF16)
    for ty in range(3):
        for tx in range(3):
            column = []
            for f in range(3):
                block = jnp.zeros((16, 1024), F32)
                for tz in range(3):
                    row = ((tx * 3 + ty) * 3 + tz) * 3 + f
                    block = jnp.where(hits[tz], win_ref[row : row + 1, :], block)
                column.append(block)
            column.append(jnp.zeros((16, 1024), F32))
            block = jnp.concatenate(column, axis=0).astype(BF16)
            for out in range(2):
                at = ty * 256 + (tx + out) * 64
                r1_ref[at : at + 64, out * 1024 : out * 1024 + 1024] = block
        r1_ref[ty * 256 + 192 : ty * 256 + 256, 0:1024] = blank
        r1_ref[ty * 256 : ty * 256 + 64, 1024:2048] = blank
    low = lax.broadcasted_iota(I32, (384, 128), 1) < 64
    for tap in range(9):
        turned = wmid_ref[tap].astype(F32)
        shifted = []
        for j in range(4):
            pieces = [turned]
            if j:
                pieces = [jnp.zeros((64 * j, 128), F32)] + pieces
            if j < 3:
                pieces = pieces + [jnp.zeros((192 - 64 * j, 128), F32)]
            shifted.append(jnp.concatenate(pieces, axis=0))
        for h in range(2):
            a, b = shifted[2 * h], shifted[2 * h + 1]
            rows = slice(tap * 384, tap * 384 + 384)
            r2_ref[0, rows, h * 128 : h * 128 + 128] = jnp.where(low, b, a).astype(BF16)
            r2_ref[1, rows, h * 128 : h * 128 + 128] = jnp.where(low, a, b).astype(BF16)
    low = lax.broadcasted_iota(I32, (64, 128), 1) < 64
    none = jnp.zeros((64, 128), BF16)
    for tap in range(9):
        w01 = wout_ref[tap, :, 0:128].astype(F32)
        w2_ = wout_ref[tap, :, 128:256].astype(F32)
        w10 = pltpu.roll(w01, 64, axis=1)
        w_2 = pltpu.roll(w2_, 64, axis=1)
        zero = jnp.zeros((64, 128), F32)
        table = [
            [w01, w_2, None],
            [jnp.where(low, zero, w10), jnp.where(low, w2_, w01), None],
            [None, w10, w2_],
            [None, jnp.where(low, w01, zero), jnp.where(low, w10, w_2)],
        ]
        for j in range(4):
            for t in range(3):
                at = tap * 384 + t * 128
                piece = table[j][t]
                w3_ref[64 * j : 64 * j + 64, at : at + 128] = none if piece is None else piece.astype(BF16)


def weights(win, wmid, wout):
    return pl.pallas_call(
        weights_kernel,
        out_shape=(
            jax.ShapeDtypeStruct((768, 2048), BF16),
            jax.ShapeDtypeStruct((2, K_TAPS, 256), BF16),
            jax.ShapeDtypeStruct((256, K_TAPS), BF16),
        ),
        name="weights",
    )(win, wmid, wout)


def layers_kernel(
    left_ref, right_ref, xl_ref, xr_ref, top_ref, bottom_ref, r1_ref, r2_ref, w3_ref,
    out_ref, ext_ref, v1_ref, tmp_ref, first_ref, second_ref, third_ref,
):
    ext_ref[:, 144:160] = jnp.zeros((8, 16, 128), F32)
    ext_ref[:, 0:8] = top_ref[...].astype(F32)
    ext_ref[:, 136:144] = bottom_ref[...].astype(F32)
    for at, source in enumerate((xl_ref, left_ref, right_ref, xr_ref)):
        ext_ref[2 * at : 2 * at + 2, 8:136] = source[...].astype(F32)
    for ty in range(3):
        for pair in range(8):
            v1_ref[ty, pair * Y1 : pair * Y1 + Y1] = ext_ref[pair, 4 + ty : 4 + ty + Y1].astype(BF16)
    tmp_ref[:, :, Y1:152] = jnp.zeros((2, 7, 8, 128), F32)

    def first_columns(column, carry):
        lhs = jnp.concatenate(
            [v1_ref[ty, p * Y1 : p * Y1 + 7 * Y1] for ty in range(3) for p in range(2)], axis=1
        )
        at = pl.multiple_of(column * 256, 256)
        u = leaky(dot(lhs, r1_ref[:, pl.ds(at, 256)]))
        for h in range(2):
            tmp_ref[h, :, 0:Y1] = u[:, h * 128 : h * 128 + 128].reshape(7, Y1, 128)
        out = column // 4
        for h in range(2):
            tile = (column % 4) * 2 + h
            for m in range(7):
                row = pl.multiple_of((2 * m + out) * Y1, Y1)
                for s in range(3):
                    first_ref[s, tile, pl.ds(row, Y1)] = tmp_ref[h, m, 2 * s : 2 * s + Y1].astype(BF16)
        return carry

    lax.fori_loop(0, 8, first_columns, 0)

    low = lax.broadcasted_iota(I32, (5 * Y1, 128), 1) < 64

    def second_rows(step, carry):
        group = step // 2
        b = step % 2
        outs = []
        for parity in range(2):
            pieces = []
            for tx in range(3):
                row = pl.multiple_of((group * 5 + 2 * tx) * Y1, Y1)
                for ty in range(3):
                    for w in range(3):
                        tile = parity * 4 + (2 * b + w) % 4
                        pieces.append(first_ref[ty, tile, pl.ds(row, 5 * Y1)])
            outs.append(leaky(dot(jnp.concatenate(pieces, axis=1), r2_ref[parity])))
        even, odd = outs
        for h in range(2):
            e = even[:, h * 128 : h * 128 + 128]
            o = odd[:, h * 128 : h * 128 + 128]
            for k, merged in enumerate((jnp.where(low, o, e), jnp.where(low, e, o))):
                tmp_ref[k, 0:5, 0:Y1] = merged.reshape(5, Y1, 128)
            for k in range(2):
                tile = 4 * b + 2 * h + k
                for q in range(5):
                    row = pl.multiple_of((group * 5 + q) * 128, 128)
                    for s in range(3):
                        second_ref[s, tile, pl.ds(row, 128)] = tmp_ref[k, q, s : s + 128].astype(BF16)
        return carry

    lax.fori_loop(0, 4, second_rows, 0)

    def third_planes(b, carry):
        for pair in range(4):
            pieces = []
            for tx in range(3):
                row = (2 * pair + tx) * 128
                for ty in range(3):
                    for w in range(3):
                        tile = (2 * b + w) % 8
                        pieces.append(second_ref[ty, tile, row : row + 256])
            u = leaky(dot(w3_ref[...], jnp.concatenate(pieces, axis=1), NT))
            for j in range(4):
                for k in range(2):
                    third_ref[j, pl.ds(2 * pair + k, 64, stride=8), :] = (
                        u[64 * j : 64 * j + 64, k * 128 : k * 128 + 128]
                    )
        for j in range(4):
            out_ref[4 * b + j] = third_ref[j].astype(BF16)
        return carry

    lax.fori_loop(0, 4, third_planes, 0)


def layers(left, right, xl, xr, top, bottom, r1, r2, w3):
    return pl.pallas_call(
        layers_kernel,
        out_shape=jax.ShapeDtypeStruct((16, 512, 128), BF16),
        scratch_shapes=[
            VMEM((8, 160, 128), F32),
            VMEM((3, 8 * Y1, 128), BF16),
            VMEM((2, 7, 152, 128), F32),
            VMEM((3, 8, 14 * Y1, 128), BF16),
            VMEM((3, 8, 10 * 128, 128), BF16),
            VMEM((4, 512, 128), F32),
        ],
        compiler_params=pltpu.CompilerParams(vmem_limit_bytes=60 << 20),
        name="layers",
    )(left, right, xl, xr, top, bottom, r1, r2, w3)


def twiddle_rows(count):
    position = np.arange(count, dtype=np.int64)
    phase = position[:, None] * position[None, :] % count
    angle = phase.astype(np.float32) * np.float32(2.0 * math.pi / count)
    factor = np.float32(1.0 / math.sqrt(count))
    parts = np.stack([np.cos(angle) * factor, -np.sin(angle) * factor])
    parts = parts.reshape(2 * count, count // 8, 8)
    table = np.zeros((2, 2 * count, count // 8, 2, 8), np.float32)
    for parity in range(2):
        table[parity, :, :, parity, :] = parts
    return table.reshape(4 * count, 2 * count)


def transform_kernel(twiddle_ref, in_ref, out_ref):
    for pair in range(2):
        rhs = jnp.concatenate(
            [
                in_ref[:, (2 * pair + k) * 16 : (2 * pair + k) * 16 + 16].reshape(256, 128)
                for k in range(2)
            ],
            axis=1,
        )
        u = dot(twiddle_ref[...], rhs).astype(BF16)
        for k in range(2):
            for parity in range(2):
                for t in range(2):
                    at = (parity * 2 + t) * 128
                    out_ref[t, 4 * pair + 2 * k + parity, 0] = u[at : at + 128, k * 128 : k * 128 + 128]


def transform(twiddle, moved):
    return pl.pallas_call(
        transform_kernel,
        grid=(8,),
        in_specs=[
            pl.BlockSpec((512, 256), lambda i: (0, 0)),
            pl.BlockSpec((16, 64, 128), lambda i: (0, i, 0)),
        ],
        out_specs=pl.BlockSpec((2, 8, 1, 128, 128), lambda i: (0, i, 0, 0, 0)),
        out_shape=jax.ShapeDtypeStruct((2, 64, 1, 128, 128), BF16),
        name="transform",
    )(twiddle, moved)


def on_device(particle_values, destination, cell_index, weight_in, weight_mid, weight_out):
    count_x = lax.axis_size("bx")
    count_y = lax.axis_size("by")
    up_x = [(i, (i + 1) % count_x) for i in range(count_x)]
    down_x = [((i + 1) % count_x, i) for i in range(count_x)]
    up_y = [(i, (i + 1) % count_y) for i in range(count_y)]
    down_y = [((i + 1) % count_y, i) for i in range(count_y)]

    outgoing = pack(destination.reshape(1, -1), cell_index.reshape(1, -1), particle_values)
    incoming = lax.all_to_all(outgoing, ("bx", "by"), split_axis=0, concat_axis=0, tiled=True)

    win = jnp.transpose(weight_in.reshape(9, 64, 9), (0, 2, 1)).reshape(81, 64)
    win = jnp.tile(win.astype(F32), (1, 16))
    wmid = jnp.transpose(weight_mid.reshape(9, 64, 192), (0, 2, 1))
    wmid = jnp.concatenate([wmid, wmid], axis=2)
    wout = jnp.pad(weight_out.reshape(9, 64, 192), ((0, 0), (0, 0), (0, 64)))
    r1, r2, w3 = weights(win, wmid, wout)

    left, right = paint(incoming)
    xl = lax.ppermute(right, "bx", up_x)
    xr = lax.ppermute(left, "bx", down_x)
    columns = (xl, left, right, xr)
    top = lax.ppermute(jnp.concatenate([c[:, 120:128] for c in columns], axis=0), "by", up_y)
    bottom = lax.ppermute(jnp.concatenate([c[:, 0:8] for c in columns], axis=0), "by", down_y)

    third = layers(left, right, xl, xr, top, bottom, r1, r2, w3)
    moved = lax.all_to_all(third, "bx", split_axis=0, concat_axis=0, tiled=True)
    twiddle = jnp.asarray(twiddle_rows(count_x * 8), BF16)
    return transform(twiddle, moved)


def solution(mesh):
    placed = (P(None, ("bx", "by")), P(("bx", "by"), None), P(("bx", "by")), P(), P(), P())
    return jax.shard_map(
        on_device,
        mesh=mesh,
        in_specs=placed,
        out_specs=P(None, None, "bx", None, "by"),
        check_vma=False,
    )
```

time: 481 us -> 121 us (0.25); the launches traced: 476 us -> 121 us
  other arithmetic: 161 us -> 1.06 us
  matrix products: 156 us -> 0 us
  Pallas kernels: 0 us -> 51 us
  local copies, waits for them, and re-layouts: 55.7 us -> 5.79 us
  waiting for transfers between devices: 58.4 us -> 15.4 us
  blocking collectives: 0 us -> 31.1 us
  starting transfers between devices: 43.9 us -> 16.1 us
    dot_general x34 -> x0, matrix products: 156 us -> none  [the longest x27 145 us: convolve(): jnp.einsum('oc,czxy->ozxy', weight[step_x, step_y], window, preferred_ele...]
    concatenate x9 -> x3, other arithmetic: 155 us -> 1.06 us  [the longest x1 1.04 us: on_device(): wmid = jnp.concatenate([wmid, wmid], axis=2)]
    pallas_call x0 -> x5, Pallas kernels: none -> 51 us  [the longest x1 33.1 us: layers(): pl.pallas_call(layers_kernel, out_shape=jax.ShapeDtypeStruct((16, 512, 12...]
    slice x16 -> x3, local copies, waits for them, and re-layouts: 36.1 us -> 0.72 us  [on_device(): c[:, 0:8]]
    all_to_all x0 -> x1, blocking collectives: none -> 31.1 us  [on_device(): moved = lax.all_to_all(third, 'bx', split_axis=0, concat_axis=0, tiled=True)]
    all_to_all x1 -> x0, waiting for transfers between devices: 28.5 us -> none  [on_device(): lax.all_to_all(current, 'bx', split_axis=1, concat_axis=2, tiled=True)]
    ppermute x12 -> x4, starting transfers between devices: 26.3 us -> 4.98 us  [the longest x1 2.93 us: on_device(): lax.ppermute(jnp.concatenate([c[:, 0:8] for c in columns], axis=0), 'by',...]
    ppermute x12 -> x4, waiting for transfers between devices: 20.5 us -> 7.16 us  [the longest x1 5.42 us: on_device(): xl = lax.ppermute(right, 'bx', up_x)]
  transfers between devices with their start and end apart: 14 -> 5, of which waited for: 6 -> 3; matrix products, arithmetic and copies ran while one was open for 2% -> 5% of each run, Pallas kernels for 0% -> 4%
where the time goes in v1:
time: 121 us
  Pallas kernels  51 us (42%)
  blocking collectives  31.1 us (26%)
  starting transfers between devices  16.1 us (13%)
  waiting for transfers between devices  15.4 us (13%)
  local copies, waits for them, and re-layouts  5.79 us (5%)
    pallas_call x1, Pallas kernels, layers(): pl.pallas_call(layers_kernel, out_shape=jax.ShapeDtypeStruct((16, 512, 12...  33.1 us
    all_to_all x1, blocking collectives, on_device(): moved = lax.all_to_all(third, 'bx', split_axis=0, concat_axis=0, tiled=True)  31.1 us
    all_to_all x1, starting transfers between devices, on_device(): lax.all_to_all(outgoing, ('bx', 'by'), split_axis=0, concat_axis=0, tiled...  11.2 us
    all_to_all x1, waiting for transfers between devices, on_device(): lax.all_to_all(outgoing, ('bx', 'by'), split_axis=0, concat_axis=0, tiled...  8.25 us
    pallas_call x1, Pallas kernels, transform(): pl.pallas_call(transform_kernel, grid=(8,), in_specs=[pl.BlockSpec((512,...  7.12 us
    ppermute x1, waiting for transfers between devices, on_device(): xl = lax.ppermute(right, 'bx', up_x)  5.42 us
    pallas_call x1, Pallas kernels, weights(): pl.pallas_call(weights_kernel, out_shape=(jax.ShapeDtypeStruct((768, 2048...  5.28 us
    ppermute x1, starting transfers between devices, on_device(): lax.ppermute(jnp.concatenate([c[:, 0:8] for c in columns], axis=0), 'by',...  2.93 us
  transfers between devices with their start and end apart: 5, of which 3 were waited for; matrix products, arithmetic and copies ran while one was open for 5% of the time, Pallas kernels for 4%

profile of v1, /device:TPU:0, one launch (start us, length us, event | category | flops | bytes accessed | tf_op | source)
XLA Modules:
  0.0 120.6 jit_solution(3531835191464451093)
XLA Ops:
  0.0 2.7 %pack.1 = f32[128,128]{1,0:T(8,128)} custom-call(s32[1,2048]{1,0:T(1,128)} %bitcast.20, s32[1,2048]{1,0:T(1,128)} %bitcast.21, f32[3,2048]{1,0:T(4,128)} %value_ref.1), custom_call_target="tpu_custom_call" | custom-call | tf_op jit(solution)/shard_map/pack/pallas_call | solution.py:66
  2.7 11.2 %all-to-all-start = ((f32[128,1,128]{2,1,0:T(1,128)}), f32[128,1,128]{2,1,0:T(1,128)S(1)}, u32[]{:S(2)}, u32[]{:S(2)}) async-start(f32[128,1,128]{2,1,0:T(1,128)} %bitcast.18), calls=%async_computation | async-start | bytes 131072 | tf_op jit(solution)/shard_map/all_to_all | solution.py:350
  13.8 1.2 %copy.18 = bf16[3,3,64,192]{2,3,1,0:T(8,128)(2,1)S(1)} copy(bf16[3,3,64,192]{3,2,1,0:T(8,128)(2,1)} %param.11) | data formatting | bytes 442368 | tf_op args[4]
  15.1 8.2 %all-to-all-done = f32[128,1,128]{2,1,0:T(1,128)S(1)} async-done(((f32[128,1,128]{2,1,0:T(1,128)}), f32[128,1,128]{2,1,0:T(1,128)S(1)}, u32[]{:S(2)}, u32[]{:S(2)}) %all-to-all-start) | async-done | bytes 65568 | tf_op jit(solution)/shard_map/all_to_all | solution.py:350
  23.3 0.6 copy-done.1
  23.9 2.8 %paint.1 = (bf16[2,128,128]{2,1,0:T(8,128)(2,1)}, bf16[2,128,128]{2,1,0:T(8,128)(2,1)}) custom-call(f32[128,128]{1,0:T(8,128)} %bitcast.19), custom_call_target="tpu_custom_call" | custom-call | tf_op jit(solution)/shard_map/paint/pallas_call | solution.py:113
  26.8 1.4 %collective-permute-start.1 = (bf16[2,128,128]{2,1,0:T(8,128)(2,1)}, bf16[2,128,128]{2,1,0:T(8,128)(2,1)S(1)}, u32[]{:S(2)}, u32[]{:S(2)}) collective-permute-start(bf16[2,128,128]{2,1,0:T(8,128)(2,1)} %get-tuple-element.10.left_ref), channel_id=1, source_target_pairs={{8,0},{16,8},{24,16},{32,24},{40,32},{48,40},{56,48},{64,56},{72,6... | collective-permute-start | bytes 196616 | tf_op jit(solution)/shard_map/ppermute | solution.py:361
  28.2 0.7 fusion.1
  28.9 0.6 collective-permute-start
  29.5 1.7 %collective-permute-done.1.xr_ref = bf16[2,128,128]{2,1,0:T(8,128)(2,1)S(1)} collective-permute-done((bf16[2,128,128]{2,1,0:T(8,128)(2,1)}, bf16[2,128,128]{2,1,0:T(8,128)(2,1)S(1)}, u32[]{:S(2)}, u32[]{:S(2)}) %collective-permute-start.1) | collective-permute-done | bytes 65568 | tf_op jit(solution)/shard_map/ppermute | solution.py:361
  31.3 5.4 %collective-permute-done.xl_ref = bf16[2,128,128]{2,1,0:T(8,128)(2,1)S(1)} collective-permute-done((bf16[2,128,128]{2,1,0:T(8,128)(2,1)}, bf16[2,128,128]{2,1,0:T(8,128)(2,1)S(1)}, u32[]{:S(2)}, u32[]{:S(2)}) %collective-permute-start) | collective-permute-done | bytes 65568 | tf_op jit(solution)/shard_map/ppermute | solution.py:360
  36.7 0.0 collective-permute-start.2
  36.7 2.9 %collective-permute-start.3 = (bf16[8,8,128]{2,1,0:T(8,128)(2,1)S(1)}, bf16[8,8,128]{2,1,0:T(8,128)(2,1)S(1)}, u32[]{:S(2)}, u32[]{:S(2)}) collective-permute-start(bf16[8,8,128]{2,1,0:T(8,128)(2,1)S(1)} %pad_maximum_fusion.2), channel_id=1, source_target_pairs={{1,0},{2,1},{3,2},{4,3},{5,4},{6,5},{7,6},{0,7},{9,8},{10,9},{11,1... | collective-permute-start | bytes 49160 | tf_op jit(solution)/shard_map/ppermute | solution.py:364
  39.7 1.0 pad_maximum_fusion.wmid_ref
  40.7 0.8 copy.15
  41.5 0.1 copy.17
  41.6 0.1 tile.4
  41.7 1.0 copy.19.win_ref
  42.6 0.8 pad.4.wout_ref
  43.4 5.3 %weights.1 = (bf16[768,2048]{1,0:T(8,128)(2,1)}, bf16[2,3456,256]{2,1,0:T(8,128)(2,1)}, bf16[256,3456]{1,0:T(8,128)(2,1)}) custom-call(f32[81,1024]{1,0:T(8,128)} %copy.19.win_ref, bf16[9,192,128]{2,1,0:T(8,128)(2,1)} %pad_maximum_fusion.wmid_ref, bf16[9,64,256]{2,1,0:T(8,128)(2,1)} %pad.4.wout_ref), custom_call_target="tpu_custom_call" | custom-call | tf_op jit(solution)/shard_map/weights/pallas_call | solution.py:183
  48.7 0.6 copy-done.4
  49.3 33.1 %layers.1 = bf16[16,512,128]{2,1,0:T(8,128)(2,1)} custom-call(bf16[2,128,128]{2,1,0:T(8,128)(2,1)} %get-tuple-element.10.left_ref, bf16[2,128,128]{2,1,0:T(8,128)(2,1)} %get-tuple-element.11.right_ref, bf16[2,128,128]{2,1,0:T(8,128)(2,1)} %copy-done.3, bf16[2,128,128]{2,1,0:T(8,128)(2,1)} %copy-done.2, bf16[8,8,128]{2,1,0:T(8,128)(2,1)} %copy-done.4, ...), custom_call_target="tpu_custom_call" | custom-call | tf_op jit(solution)/shard_map/layers/pallas_call | solution.py:281
  82.4 31.1 %all_to_all.16.in_ref = bf16[16,512,128]{2,1,0:T(8,128)(2,1)} all-to-all(bf16[16,512,128]{2,1,0:T(8,128)(2,1)} %layers.1), channel_id=1, replica_groups=mesh['bx'=16,'by'=8] {'bx'}, dimensions={0} | all-to-all | bytes 4194304 | tf_op jit(solution)/shard_map/all_to_all | solution.py:367
  113.4 7.1 %transform.1 = bf16[2,64,1,128,128]{4,3,2,1,0:T(8,128)(2,1)} custom-call(bf16[512,256]{1,0:T(8,128)(2,1)} %constant.5.clone.twiddle_ref, bf16[16,512,128]{2,1,0:T(8,128)(2,1)} %all_to_all.16.in_ref), custom_call_target="tpu_custom_call" | custom-call | tf_op jit(solution)/shard_map/transform/pallas_call | solution.py:328
  (19 shorter events, 0.1 us)
Async XLA Ops:
  0.0 42.6 %copy-start = (bf16[3,3,64,192]{3,2,1,0:T(8,128)(2,1)S(1)}, bf16[3,3,64,192]{3,2,1,0:T(8,128)(2,1)}, u32[]{:S(2)}) copy-start(bf16[3,3,64,192]{3,2,1,0:T(8,128)(2,1)} %param.12) | copy-start | bytes 663556
  2.7 20.6 %all-to-all-start = ((f32[128,1,128]{2,1,0:T(1,128)}), f32[128,1,128]{2,1,0:T(1,128)S(1)}, u32[]{:S(2)}, u32[]{:S(2)}) async-start(f32[128,1,128]{2,1,0:T(1,128)} %bitcast.18), calls=%async_computation | async-start | bytes 131072 | tf_op jit(solution)/shard_map/all_to_all | solution.py:350
  23.3 0.6 copy-start.1
  26.8 4.5 %collective-permute-start.1 = (bf16[2,128,128]{2,1,0:T(8,128)(2,1)}, bf16[2,128,128]{2,1,0:T(8,128)(2,1)S(1)}, u32[]{:S(2)}, u32[]{:S(2)}) collective-permute-start(bf16[2,128,128]{2,1,0:T(8,128)(2,1)} %get-tuple-element.10.left_ref), channel_id=1, source_target_pairs={{8,0},{16,8},{24,16},{32,24},{40,32},{48,40},{56,48},{64,56},{72,6... | collective-permute-start | bytes 196616 | tf_op jit(solution)/shard_map/ppermute | solution.py:361
  28.9 7.8 %collective-permute-start = (bf16[2,128,128]{2,1,0:T(8,128)(2,1)}, bf16[2,128,128]{2,1,0:T(8,128)(2,1)S(1)}, u32[]{:S(2)}, u32[]{:S(2)}) collective-permute-start(bf16[2,128,128]{2,1,0:T(8,128)(2,1)} %get-tuple-element.11.right_ref), channel_id=1, source_target_pairs={{0,8},{8,16},{16,24},{24,32},{32,40},{40,48},{48,56},{56,64},{64,7... | collective-permute-start | bytes 196616 | tf_op jit(solution)/shard_map/ppermute | solution.py:360
  31.3 17.4 %copy-start.2 = (bf16[2,128,128]{2,1,0:T(8,128)(2,1)}, bf16[2,128,128]{2,1,0:T(8,128)(2,1)S(1)}, u32[]{:S(2)}) copy-start(bf16[2,128,128]{2,1,0:T(8,128)(2,1)S(1)} %collective-permute-done.1.xr_ref) | copy-start | bytes 196612
  36.7 12.0 %copy-start.3 = (bf16[2,128,128]{2,1,0:T(8,128)(2,1)}, bf16[2,128,128]{2,1,0:T(8,128)(2,1)S(1)}, u32[]{:S(2)}) copy-start(bf16[2,128,128]{2,1,0:T(8,128)(2,1)S(1)} %collective-permute-done.xl_ref) | copy-start | bytes 196612
  36.7 12.0 %collective-permute-start.2 = (bf16[8,8,128]{2,1,0:T(8,128)(2,1)S(1)}, bf16[8,8,128]{2,1,0:T(8,128)(2,1)S(1)}, u32[]{:S(2)}, u32[]{:S(2)}) collective-permute-start(bf16[8,8,128]{2,1,0:T(8,128)(2,1)S(1)} %pad_maximum_fusion.1), channel_id=1, source_target_pairs={{0,1},{1,2},{2,3},{3,4},{4,5},{5,6},{6,7},{7,0},{8,9},{9,10},{10,1... | collective-permute-start | bytes 49160 | tf_op jit(solution)/shard_map/ppermute | solution.py:363
  36.7 11.9 %collective-permute-start.3 = (bf16[8,8,128]{2,1,0:T(8,128)(2,1)S(1)}, bf16[8,8,128]{2,1,0:T(8,128)(2,1)S(1)}, u32[]{:S(2)}, u32[]{:S(2)}) collective-permute-start(bf16[8,8,128]{2,1,0:T(8,128)(2,1)S(1)} %pad_maximum_fusion.2), channel_id=1, source_target_pairs={{1,0},{2,1},{3,2},{4,3},{5,4},{6,5},{7,6},{0,7},{9,8},{10,9},{11,1... | collective-permute-start | bytes 49160 | tf_op jit(solution)/shard_map/ppermute | solution.py:364
  48.7 0.6 copy-start.4
  48.7 0.6 copy-start.5

commit v2 on v1

--- a/solution.py
+++ b/solution.py
@@ -70,7 +70,10 @@
     )(dest, cell, values)
 
 
-def paint_kernel(in_ref, left_ref, right_ref, acc_ref):
+def paint_kernel(in_any, after_any, left_ref, right_ref, acc_ref, in_ref, sem):
+    copy = pltpu.make_async_copy(in_any, in_ref, sem)
+    copy.start()
+    copy.wait()
     turned = jnp.transpose(in_ref[...], (1, 0))
     cells = turned[0:32].astype(I32)
     place = ((cells >> 8) & 3) * 128 + (cells & 127)
@@ -108,94 +111,109 @@
     right_ref[...] = painted[256:].reshape(2, 128, 128)
 
 
-def paint(incoming):
+def paint(incoming, after):
     half = jax.ShapeDtypeStruct((2, 128, 128), BF16)
     return pl.pallas_call(
         paint_kernel,
+        in_specs=[pl.BlockSpec(memory_space=pl.ANY)] * 2,
         out_shape=(half, half),
-        scratch_shapes=[VMEM((512, 256), F32)],
+        scratch_shapes=[VMEM((512, 256), F32), VMEM((128, 128), F32), pltpu.SemaphoreType.DMA(())],
         name="paint",
-    )(incoming)
-
-
-def weights_kernel(win_ref, wmid_ref, wout_ref, r1_ref, r2_ref, w3_ref):
-    lane = lax.broadcasted_iota(I32, (16, 1024), 1)
-    tile = lane // 128
-    half = (lane // 64) % 2
-    z_out = jnp.where(tile < 4, 14 + 4 * tile + 2 * half, 13 + 4 * (tile - 4) + 2 * half) % 16
-    tap_z = (lax.broadcasted_iota(I32, (16, 1024), 0) - z_out + 17) % 16
-    hits = [tap_z == tz for tz in range(3)]
-    blank = jnp.zeros((64, 1024), BF16)
+    )(incoming, after)
+
+
+def weights_kernel(win_ref, wmid_ref, wout_ref, r1_ref, w2_ref, w3_ref):
+    lane = lax.broadcasted_iota(I32, (16, 128), 1)
+    depth = lax.broadcasted_iota(I32, (16, 128), 0)
+    blank = jnp.zeros((16, 128), F32)
+    hits = []
+    for tile in range(8):
+        first_z = 14 + 4 * tile if tile < 4 else 13 + 4 * (tile - 4)
+        tap_z = (depth - first_z - 2 * (lane // 64) + 49) % 16
+        hits.append([tap_z == tz for tz in range(3)])
+    for tx in range(3):
+        for ty in range(3):
+            rows = [
+                [
+                    jnp.broadcast_to(
+                        jnp.concatenate([win_ref[tx, tz * 3 + f, ty : ty + 1, :].astype(F32)] * 2, axis=1),
+                        (16, 128),
+                    )
+                    for tz in range(3)
+                ]
+                for f in range(3)
+            ]
+            for tile in range(8):
+                column = []
+                for f in range(3):
+                    block = blank
+                    for tz in range(3):
+                        block = jnp.where(hits[tile][tz], rows[f][tz], block)
+                    column.append(block)
+                block = jnp.concatenate(column + [blank], axis=0).astype(BF16)
+                for out in range(2):
+                    at = ty * 256 + (tx + out) * 64
+                    r1_ref[out * 8 + tile, at : at + 64] = block
+    none = jnp.zeros((64, 128), BF16)
     for ty in range(3):
-        for tx in range(3):
-            column = []
-            for f in range(3):
-                block = jnp.zeros((16, 1024), F32)
-                for tz in range(3):
-                    row = ((tx * 3 + ty) * 3 + tz) * 3 + f
-                    block = jnp.where(hits[tz], win_ref[row : row + 1, :], block)
-                column.append(block)
-            column.append(jnp.zeros((16, 1024), F32))
-            block = jnp.concatenate(column, axis=0).astype(BF16)
-            for out in range(2):
-                at = ty * 256 + (tx + out) * 64
-                r1_ref[at : at + 64, out * 1024 : out * 1024 + 1024] = block
-        r1_ref[ty * 256 + 192 : ty * 256 + 256, 0:1024] = blank
-        r1_ref[ty * 256 : ty * 256 + 64, 1024:2048] = blank
-    low = lax.broadcasted_iota(I32, (384, 128), 1) < 64
-    for tap in range(9):
-        turned = wmid_ref[tap].astype(F32)
-        shifted = []
-        for j in range(4):
-            pieces = [turned]
-            if j:
-                pieces = [jnp.zeros((64 * j, 128), F32)] + pieces
-            if j < 3:
-                pieces = pieces + [jnp.zeros((192 - 64 * j, 128), F32)]
-            shifted.append(jnp.concatenate(pieces, axis=0))
-        for h in range(2):
-            a, b = shifted[2 * h], shifted[2 * h + 1]
-            rows = slice(tap * 384, tap * 384 + 384)
-            r2_ref[0, rows, h * 128 : h * 128 + 128] = jnp.where(low, b, a).astype(BF16)
-            r2_ref[1, rows, h * 128 : h * 128 + 128] = jnp.where(low, a, b).astype(BF16)
+        for tile in range(8):
+            r1_ref[tile, ty * 256 + 192 : ty * 256 + 256] = none
+            r1_ref[8 + tile, ty * 256 : ty * 256 + 64] = none
     low = lax.broadcasted_iota(I32, (64, 128), 1) < 64
-    none = jnp.zeros((64, 128), BF16)
-    for tap in range(9):
-        w01 = wout_ref[tap, :, 0:128].astype(F32)
-        w2_ = wout_ref[tap, :, 128:256].astype(F32)
-        w10 = pltpu.roll(w01, 64, axis=1)
-        w_2 = pltpu.roll(w2_, 64, axis=1)
-        zero = jnp.zeros((64, 128), F32)
-        table = [
-            [w01, w_2, None],
-            [jnp.where(low, zero, w10), jnp.where(low, w2_, w01), None],
-            [None, w10, w2_],
-            [None, jnp.where(low, w01, zero), jnp.where(low, w10, w_2)],
-        ]
-        for j in range(4):
-            for t in range(3):
-                at = tap * 384 + t * 128
-                piece = table[j][t]
-                w3_ref[64 * j : 64 * j + 64, at : at + 128] = none if piece is None else piece.astype(BF16)
+    zero = jnp.zeros((64, 128), F32)
+    for source, target, swap in ((wmid_ref, w2_ref, False), (wout_ref, w3_ref, True)):
+        for tap in range(9):
+            w01 = source[tap // 3, tap % 3, :, 0:128].astype(F32)
+            w2_ = jnp.concatenate(
+                [source[tap // 3, tap % 3, :, 128:192].astype(F32), jnp.zeros((64, 64), F32)], axis=1
+            )
+            w10 = pltpu.roll(w01, 64, axis=1)
+            w_2 = pltpu.roll(w2_, 64, axis=1)
+            w_0 = jnp.where(low, zero, w10)
+            w12 = jnp.where(low, w10, w_2)
+            if swap:
+                table = [
+                    [w01, w_2, None],
+                    [w_0, jnp.where(low, w2_, w01), None],
+                    [None, w10, w2_],
+                    [None, jnp.where(low, w01, zero), w12],
+                ]
+            else:
+                table = [[w01, w2_, None], [w_0, w12, None], [None, w01, w2_], [None, w_0, w12]]
+            for j in range(4):
+                for t in range(3):
+                    piece = table[j][t]
+                    target[tap * 3 + t, 64 * j : 64 * j + 64] = none if piece is None else piece.astype(BF16)
 
 
 def weights(win, wmid, wout):
     return pl.pallas_call(
         weights_kernel,
         out_shape=(
-            jax.ShapeDtypeStruct((768, 2048), BF16),
-            jax.ShapeDtypeStruct((2, K_TAPS, 256), BF16),
-            jax.ShapeDtypeStruct((256, K_TAPS), BF16),
+            jax.ShapeDtypeStruct((16, 768, 128), BF16),
+            jax.ShapeDtypeStruct((27, 256, 128), BF16),
+            jax.ShapeDtypeStruct((27, 256, 128), BF16),
         ),
         name="weights",
     )(win, wmid, wout)
 
 
 def layers_kernel(
-    left_ref, right_ref, xl_ref, xr_ref, top_ref, bottom_ref, r1_ref, r2_ref, w3_ref,
-    out_ref, ext_ref, v1_ref, tmp_ref, first_ref, second_ref, third_ref,
+    left_ref, right_ref, xl_any, xr_any, top_any, bottom_any, r1_any, w2_any, w3_any, out_any,
+    xl_ref, xr_ref, top_ref, bottom_ref, r1_ref, w2_ref, w3_ref,
+    ext_ref, v1_ref, tmp_ref, first_ref, second_ref, rows_ref, third_ref, out_ref, in_sem, out_sem,
 ):
+    pairs = (
+        (xl_any, xl_ref), (xr_any, xr_ref), (top_any, top_ref), (bottom_any, bottom_ref),
+        (r1_any, r1_ref), (w2_any, w2_ref), (w3_any, w3_ref),
+    )
+    copies = [pltpu.make_async_copy(a, b, in_sem.at[i]) for i, (a, b) in enumerate(pairs)]
+    for copy in copies:
+        copy.start()
     ext_ref[:, 144:160] = jnp.zeros((8, 16, 128), F32)
+    tmp_ref[:, :, Y1:152] = jnp.zeros((2, 7, 8, 128), F32)
+    for copy in copies[:4]:
+        copy.wait()
     ext_ref[:, 0:8] = top_ref[...].astype(F32)
     ext_ref[:, 136:144] = bottom_ref[...].astype(F32)
     for at, source in enumerate((xl_ref, left_ref, right_ref, xr_ref)):
@@ -203,14 +221,14 @@
     for ty in range(3):
         for pair in range(8):
             v1_ref[ty, pair * Y1 : pair * Y1 + Y1] = ext_ref[pair, 4 + ty : 4 + ty + Y1].astype(BF16)
-    tmp_ref[:, :, Y1:152] = jnp.zeros((2, 7, 8, 128), F32)
+    copies[4].wait()
 
     def first_columns(column, carry):
         lhs = jnp.concatenate(
             [v1_ref[ty, p * Y1 : p * Y1 + 7 * Y1] for ty in range(3) for p in range(2)], axis=1
         )
-        at = pl.multiple_of(column * 256, 256)
-        u = leaky(dot(lhs, r1_ref[:, pl.ds(at, 256)]))
+        rhs = jnp.concatenate([r1_ref[2 * column], r1_ref[2 * column + 1]], axis=1)
+        u = leaky(dot(lhs, rhs))
         for h in range(2):
             tmp_ref[h, :, 0:Y1] = u[:, h * 128 : h * 128 + 128].reshape(7, Y1, 128)
         out = column // 4
@@ -223,6 +241,7 @@
         return carry
 
     lax.fori_loop(0, 8, first_columns, 0)
+    copies[5].wait()
 
     low = lax.broadcasted_iota(I32, (5 * Y1, 128), 1) < 64
 
@@ -238,7 +257,15 @@
                     for w in range(3):
                         tile = parity * 4 + (2 * b + w) % 4
                         pieces.append(first_ref[ty, tile, pl.ds(row, 5 * Y1)])
-            outs.append(leaky(dot(jnp.concatenate(pieces, axis=1), r2_ref[parity])))
+            order = (0, 1, 2, 3) if parity else (1, 0, 3, 2)
+            rhs = jnp.concatenate(
+                [
+                    jnp.concatenate([w2_ref[k, 64 * j : 64 * j + 64] for j in order], axis=0)
+                    for k in range(27)
+                ],
+                axis=1,
+            )
+            outs.append(leaky(dot(jnp.concatenate(pieces, axis=1), rhs, NT)))
         even, odd = outs
         for h in range(2):
             e = even[:, h * 128 : h * 128 + 128]
@@ -254,44 +281,73 @@
         return carry
 
     lax.fori_loop(0, 4, second_rows, 0)
-
-    def third_planes(b, carry):
-        for pair in range(4):
-            pieces = []
-            for tx in range(3):
-                row = (2 * pair + tx) * 128
-                for ty in range(3):
-                    for w in range(3):
-                        tile = (2 * b + w) % 8
-                        pieces.append(second_ref[ty, tile, row : row + 256])
-            u = leaky(dot(w3_ref[...], jnp.concatenate(pieces, axis=1), NT))
-            for j in range(4):
+    copies[6].wait()
+
+    def third_rows(b):
+        pieces = []
+        for tx in range(3):
+            for ty in range(3):
+                for w in range(3):
+                    pieces.append(second_ref[ty, (2 * b + w) % 8, tx * 128 : tx * 128 + 1024])
+        rhs = jnp.concatenate([w3_ref[k] for k in range(27)], axis=1)
+        u = leaky(dot(jnp.concatenate(pieces, axis=1), rhs, NT))
+        for h in range(2):
+            rows_ref[b % 2, h] = u[:, h * 128 : h * 128 + 128]
+
+    def third_planes(b):
+        for x in range(8):
+            for h in range(2):
+                turned = jnp.transpose(rows_ref[b % 2, h, x * 128 : x * 128 + 128], (1, 0))
                 for k in range(2):
-                    third_ref[j, pl.ds(2 * pair + k, 64, stride=8), :] = (
-                        u[64 * j : 64 * j + 64, k * 128 : k * 128 + 128]
-                    )
+                    third_ref[2 * h + k, pl.ds(x, 64, stride=8), :] = turned[64 * k : 64 * k + 64]
         for j in range(4):
             out_ref[4 * b + j] = third_ref[j].astype(BF16)
-        return carry
-
-    lax.fori_loop(0, 4, third_planes, 0)
-
-
-def layers(left, right, xl, xr, top, bottom, r1, r2, w3):
+        copy = pltpu.make_async_copy(
+            out_ref.at[4 * b : 4 * b + 4], out_any.at[4 * b : 4 * b + 4], out_sem.at[b]
+        )
+        copy.start()
+        return copy
+
+    sent = []
+    for b in range(4):
+        third_rows(b)
+        if b:
+            sent.append(third_planes(b - 1))
+    sent.append(third_planes(3))
+    for copy in sent:
+        copy.wait()
+
+
+def layers(left, right, xl, xr, top, bottom, r1, w2, w3):
+    whole = pl.BlockSpec(memory_space=pltpu.VMEM)
+    anywhere = pl.BlockSpec(memory_space=pl.ANY)
     return pl.pallas_call(
         layers_kernel,
+        in_specs=[whole] * 2 + [anywhere] * 7,
+        out_specs=anywhere,
         out_shape=jax.ShapeDtypeStruct((16, 512, 128), BF16),
         scratch_shapes=[
+            VMEM((2, 128, 128), BF16),
+            VMEM((2, 128, 128), BF16),
+            VMEM((8, 8, 128), BF16),
+            VMEM((8, 8, 128), BF16),
+            VMEM((16, 768, 128), BF16),
+            VMEM((27, 256, 128), BF16),
+            VMEM((27, 256, 128), BF16),
             VMEM((8, 160, 128), F32),
             VMEM((3, 8 * Y1, 128), BF16),
             VMEM((2, 7, 152, 128), F32),
             VMEM((3, 8, 14 * Y1, 128), BF16),
             VMEM((3, 8, 10 * 128, 128), BF16),
+            VMEM((2, 2, 1024, 128), F32),
             VMEM((4, 512, 128), F32),
+            VMEM((16, 512, 128), BF16),
+            pltpu.SemaphoreType.DMA((7,)),
+            pltpu.SemaphoreType.DMA((4,)),
         ],
         compiler_params=pltpu.CompilerParams(vmem_limit_bytes=60 << 20),
         name="layers",
-    )(left, right, xl, xr, top, bottom, r1, r2, w3)
+    )(left, right, xl, xr, top, bottom, r1, w2, w3)
 
 
 def twiddle_rows(count):
@@ -304,11 +360,12 @@
     table = np.zeros((2, 2 * count, count // 8, 2, 8), np.float32)
     for parity in range(2):
         table[parity, :, :, parity, :] = parts
-    return table.reshape(4 * count, 2 * count)
+    return table.reshape(4 * count, 2, count).transpose(1, 0, 2)
 
 
 def transform_kernel(twiddle_ref, in_ref, out_ref):
-    for pair in range(2):
+    lhs = jnp.concatenate([twiddle_ref[0], twiddle_ref[1]], axis=1)
+    for pair in range(4):
         rhs = jnp.concatenate(
             [
                 in_ref[:, (2 * pair + k) * 16 : (2 * pair + k) * 16 + 16].reshape(256, 128)
@@ -316,7 +373,7 @@
             ],
             axis=1,
         )
-        u = dot(twiddle_ref[...], rhs).astype(BF16)
+        u = dot(lhs, rhs).astype(BF16)
         for k in range(2):
             for parity in range(2):
                 for t in range(2):
@@ -327,12 +384,12 @@
 def transform(twiddle, moved):
     return pl.pallas_call(
         transform_kernel,
-        grid=(8,),
+        grid=(4,),
         in_specs=[
-            pl.BlockSpec((512, 256), lambda i: (0, 0)),
-            pl.BlockSpec((16, 64, 128), lambda i: (0, i, 0)),
+            pl.BlockSpec((2, 512, 128), lambda i: (0, 0, 0)),
+            pl.BlockSpec((16, 128, 128), lambda i: (0, i, 0)),
         ],
-        out_specs=pl.BlockSpec((2, 8, 1, 128, 128), lambda i: (0, i, 0, 0, 0)),
+        out_specs=pl.BlockSpec((2, 16, 1, 128, 128), lambda i: (0, i, 0, 0, 0)),
         out_shape=jax.ShapeDtypeStruct((2, 64, 1, 128, 128), BF16),
         name="transform",
     )(twiddle, moved)
@@ -349,21 +406,16 @@
     outgoing = pack(destination.reshape(1, -1), cell_index.reshape(1, -1), particle_values)
     incoming = lax.all_to_all(outgoing, ("bx", "by"), split_axis=0, concat_axis=0, tiled=True)
 
-    win = jnp.transpose(weight_in.reshape(9, 64, 9), (0, 2, 1)).reshape(81, 64)
-    win = jnp.tile(win.astype(F32), (1, 16))
-    wmid = jnp.transpose(weight_mid.reshape(9, 64, 192), (0, 2, 1))
-    wmid = jnp.concatenate([wmid, wmid], axis=2)
-    wout = jnp.pad(weight_out.reshape(9, 64, 192), ((0, 0), (0, 0), (0, 64)))
-    r1, r2, w3 = weights(win, wmid, wout)
-
-    left, right = paint(incoming)
+    r1, w2, w3 = weights(jnp.transpose(weight_in, (0, 3, 1, 2)), weight_mid, weight_out)
+
+    left, right = paint(incoming, r1)
     xl = lax.ppermute(right, "bx", up_x)
     xr = lax.ppermute(left, "bx", down_x)
     columns = (xl, left, right, xr)
     top = lax.ppermute(jnp.concatenate([c[:, 120:128] for c in columns], axis=0), "by", up_y)
     bottom = lax.ppermute(jnp.concatenate([c[:, 0:8] for c in columns], axis=0), "by", down_y)
 
-    third = layers(left, right, xl, xr, top, bottom, r1, r2, w3)
+    third = layers(left, right, xl, xr, top, bottom, r1, w2, w3)
     moved = lax.all_to_all(third, "bx", split_axis=0, concat_axis=0, tiled=True)
     twiddle = jnp.asarray(twiddle_rows(count_x * 8), BF16)
     return transform(twiddle, moved)

time: 121 us -> 112 us (0.926)
  Pallas kernels: 51 us -> 46.6 us
  local copies, waits for them, and re-layouts: 5.79 us -> 1.94 us
  blocking collectives: 31.1 us -> 33.2 us
  waiting for transfers between devices: 15.4 us -> 13.4 us
    pallas_call x4, Pallas kernels: 48.3 us -> 44 us  [the longest x1 31.5 us: layers(): pl.pallas_call(layers_kernel, in_specs=[whole] * 2 + [anywhere] * 7, out_...]
    all_to_all x1, waiting for transfers between devices: 8.25 us -> 4.82 us  [on_device(): lax.all_to_all(outgoing, ('bx', 'by'), split_axis=0, concat_axis=0, tiled...]
    all_to_all x1, blocking collectives: 31.1 us -> 33.2 us  [on_device(): moved = lax.all_to_all(third, 'bx', split_axis=0, concat_axis=0, tiled=True)]
    ppermute x1, waiting for transfers between devices: 0.01 us -> 1.41 us  [on_device(): lax.ppermute(jnp.concatenate([c[:, 120:128] for c in columns], axis=0), '...]
    unnamed x13 -> x10, local copies, waits for them, and re-layouts: 2.43 us -> 1.21 us
  transfers between devices with their start and end apart: 5 -> 5, of which waited for: 3 -> 4; matrix products, arithmetic and copies ran while one was open for 5% -> 1% of each run, Pallas kernels for 4% -> 4%
where the time goes in v2:
time: 112 us
  Pallas kernels  46.6 us (42%)
  blocking collectives  33.2 us (30%)
  starting transfers between devices  16.2 us (14%)
  waiting for transfers between devices  13.4 us (12%)
  local copies, waits for them, and re-layouts  1.94 us (2%)
    all_to_all x1, blocking collectives, on_device(): moved = lax.all_to_all(third, 'bx', split_axis=0, concat_axis=0, tiled=True)  33.2 us
    pallas_call x1, Pallas kernels, layers(): pl.pallas_call(layers_kernel, in_specs=[whole] * 2 + [anywhere] * 7, out_...  31.5 us
    all_to_all x1, starting transfers between devices, on_device(): lax.all_to_all(outgoing, ('bx', 'by'), split_axis=0, concat_axis=0, tiled...  11.2 us
    ppermute x1, waiting for transfers between devices, on_device(): xl = lax.ppermute(right, 'bx', up_x)  5.43 us
    pallas_call x1, Pallas kernels, transform(): pl.pallas_call(transform_kernel, grid=(4,), in_specs=[pl.BlockSpec((2, 51...  5.01 us
    all_to_all x1, waiting for transfers between devices, on_device(): lax.all_to_all(outgoing, ('bx', 'by'), split_axis=0, concat_axis=0, tiled...  4.82 us
    pallas_call x1, Pallas kernels, weights(): pl.pallas_call(weights_kernel, out_shape=(jax.ShapeDtypeStruct((16, 768,...  4.71 us
    ppermute x1, starting transfers between devices, on_device(): lax.ppermute(jnp.concatenate([c[:, 0:8] for c in columns], axis=0), 'by',...  2.93 us
  transfers between devices with their start and end apart: 5, of which 4 were waited for; matrix products, arithmetic and copies ran while one was open for 1% of the time, Pallas kernels for 4%

profile of v2, /device:TPU:0, one launch (start us, length us, event | category | flops | bytes accessed | tf_op | source)
XLA Modules:
  0.0 111.5 jit_solution(9647226589677114589)
XLA Ops:
  0.0 2.6 %pack.1 = f32[128,128]{1,0:T(8,128)} custom-call(s32[1,2048]{1,0:T(1,128)} %bitcast.10, s32[1,2048]{1,0:T(1,128)} %bitcast.11, f32[3,2048]{1,0:T(4,128)} %value_ref.1), custom_call_target="tpu_custom_call" | custom-call | tf_op jit(solution)/shard_map/pack/pallas_call | solution.py:66
  2.6 11.2 %all-to-all-start = ((f32[128,1,128]{2,1,0:T(1,128)}), f32[128,1,128]{2,1,0:T(1,128)S(1)}, u32[]{:S(2)}, u32[]{:S(2)}) async-start(f32[128,1,128]{2,1,0:T(1,128)} %bitcast.8), calls=%async_computation | async-start | bytes 131072 | tf_op jit(solution)/shard_map/all_to_all | solution.py:407
  13.8 4.7 %weights.1 = (bf16[16,768,128]{2,1,0:T(8,128)(2,1)}, bf16[27,256,128]{2,1,0:T(8,128)(2,1)}, bf16[27,256,128]{2,1,0:T(8,128)(2,1)}) custom-call(bf16[3,9,3,64]{3,2,1,0:T(4,128)(2,1)} %bitcast.9, bf16[3,3,64,192]{3,2,1,0:T(8,128)(2,1)} %wmid_ref.1, bf16[3,3,64,192]{3,2,1,0:T(8,128)(2,1)} %wout_ref.1), custom_call_target="tpu_custom_call" | custom-call | tf_op jit(solution)/shard_map/weights/pallas_call | solution.py:190
  18.5 4.8 %all-to-all-done = f32[128,1,128]{2,1,0:T(1,128)S(1)} async-done(((f32[128,1,128]{2,1,0:T(1,128)}), f32[128,1,128]{2,1,0:T(1,128)S(1)}, u32[]{:S(2)}, u32[]{:S(2)}) %all-to-all-start) | async-done | bytes 65568 | tf_op jit(solution)/shard_map/all_to_all | solution.py:407
  23.3 0.0 copy-start
  23.3 0.6 copy-done
  23.9 2.8 %paint.1 = (bf16[2,128,128]{2,1,0:T(8,128)(2,1)}, bf16[2,128,128]{2,1,0:T(8,128)(2,1)}) custom-call(f32[128,128]{1,0:T(8,128)} %bitcast.7, bf16[16,768,128]{2,1,0:T(8,128)(2,1)} %get-tuple-element.10.after_any.r1_any), custom_call_target="tpu_custom_call" | custom-call | tf_op jit(solution)/shard_map/paint/pallas_call | solution.py:116
  26.8 1.5 %collective-permute-start.1 = (bf16[2,128,128]{2,1,0:T(8,128)(2,1)}, bf16[2,128,128]{2,1,0:T(8,128)(2,1)S(1)}, u32[]{:S(2)}, u32[]{:S(2)}) collective-permute-start(bf16[2,128,128]{2,1,0:T(8,128)(2,1)} %get-tuple-element.11.left_ref), channel_id=1, source_target_pairs={{8,0},{16,8},{24,16},{32,24},{40,32},{48,40},{56,48},{64,56},{72,6... | collective-permute-start | bytes 196616 | tf_op jit(solution)/shard_map/ppermute | solution.py:413
  28.2 0.7 fusion.1
  29.0 0.6 collective-permute-start
  29.6 1.7 %collective-permute-done.1.xr_any = bf16[2,128,128]{2,1,0:T(8,128)(2,1)S(1)} collective-permute-done((bf16[2,128,128]{2,1,0:T(8,128)(2,1)}, bf16[2,128,128]{2,1,0:T(8,128)(2,1)S(1)}, u32[]{:S(2)}, u32[]{:S(2)}) %collective-permute-start.1) | collective-permute-done | bytes 65568 | tf_op jit(solution)/shard_map/ppermute | solution.py:413
  31.3 0.0 copy-start.1
  31.3 5.4 %collective-permute-done.xl_any = bf16[2,128,128]{2,1,0:T(8,128)(2,1)S(1)} collective-permute-done((bf16[2,128,128]{2,1,0:T(8,128)(2,1)}, bf16[2,128,128]{2,1,0:T(8,128)(2,1)S(1)}, u32[]{:S(2)}, u32[]{:S(2)}) %collective-permute-start) | collective-permute-done | bytes 65568 | tf_op jit(solution)/shard_map/ppermute | solution.py:412
  36.8 0.0 collective-permute-start.2
  36.8 2.9 %collective-permute-start.3 = (bf16[8,8,128]{2,1,0:T(8,128)(2,1)S(1)}, bf16[8,8,128]{2,1,0:T(8,128)(2,1)S(1)}, u32[]{:S(2)}, u32[]{:S(2)}) collective-permute-start(bf16[8,8,128]{2,1,0:T(8,128)(2,1)S(1)} %pad_maximum_fusion.1), channel_id=1, source_target_pairs={{1,0},{2,1},{3,2},{4,3},{5,4},{6,5},{7,6},{0,7},{9,8},{10,9},{11,1... | collective-permute-start | bytes 49160 | tf_op jit(solution)/shard_map/ppermute | solution.py:416
  39.7 1.4 %collective-permute-done.2.top_any = bf16[8,8,128]{2,1,0:T(8,128)(2,1)S(1)} collective-permute-done((bf16[8,8,128]{2,1,0:T(8,128)(2,1)S(1)}, bf16[8,8,128]{2,1,0:T(8,128)(2,1)S(1)}, u32[]{:S(2)}, u32[]{:S(2)}) %collective-permute-start.2) | collective-permute-done | bytes 16416 | tf_op jit(solution)/shard_map/ppermute | solution.py:415
  41.2 0.0 collective-permute-done.3.bottom_any
  41.2 0.0 copy-done.1
  41.2 0.0 copy-done.2
  41.2 0.6 copy-done.3
  41.8 0.0 copy-done.4
  41.8 31.5 %layers.1 = bf16[16,512,128]{2,1,0:T(8,128)(2,1)} custom-call(bf16[2,128,128]{2,1,0:T(8,128)(2,1)} %get-tuple-element.11.left_ref, bf16[2,128,128]{2,1,0:T(8,128)(2,1)} %get-tuple-element.12.right_ref, bf16[2,128,128]{2,1,0:T(8,128)(2,1)} %copy-done.2, bf16[2,128,128]{2,1,0:T(8,128)(2,1)} %copy-done.1, bf16[8,8,128]{2,1,0:T(8,128)(2,1)} %copy-done.3, ...), custom_call_target="tpu_custom_call" | custom-call | tf_op jit(solution)/shard_map/layers/pallas_call | solution.py:324
  73.3 33.2 %all_to_all.16.in_ref = bf16[16,512,128]{2,1,0:T(8,128)(2,1)} all-to-all(bf16[16,512,128]{2,1,0:T(8,128)(2,1)} %layers.1), channel_id=1, replica_groups=mesh['bx'=16,'by'=8] {'bx'}, dimensions={0} | all-to-all | bytes 4194304 | tf_op jit(solution)/shard_map/all_to_all | solution.py:419
  106.5 5.0 %transform.1 = bf16[2,64,1,128,128]{4,3,2,1,0:T(8,128)(2,1)} custom-call(bf16[2,512,128]{2,1,0:T(8,128)(2,1)} %constant.2.clone.twiddle_ref, bf16[16,512,128]{2,1,0:T(8,128)(2,1)} %all_to_all.16.in_ref), custom_call_target="tpu_custom_call" | custom-call | tf_op jit(solution)/shard_map/transform/pallas_call | solution.py:385
  (7 shorter events, 0.0 us)
Async XLA Ops:
  2.6 20.7 %all-to-all-start = ((f32[128,1,128]{2,1,0:T(1,128)}), f32[128,1,128]{2,1,0:T(1,128)S(1)}, u32[]{:S(2)}, u32[]{:S(2)}) async-start(f32[128,1,128]{2,1,0:T(1,128)} %bitcast.8), calls=%async_computation | async-start | bytes 131072 | tf_op jit(solution)/shard_map/all_to_all | solution.py:407
  23.3 0.6 copy-start
  26.8 4.5 %collective-permute-start.1 = (bf16[2,128,128]{2,1,0:T(8,128)(2,1)}, bf16[2,128,128]{2,1,0:T(8,128)(2,1)S(1)}, u32[]{:S(2)}, u32[]{:S(2)}) collective-permute-start(bf16[2,128,128]{2,1,0:T(8,128)(2,1)} %get-tuple-element.11.left_ref), channel_id=1, source_target_pairs={{8,0},{16,8},{24,16},{32,24},{40,32},{48,40},{56,48},{64,56},{72,6... | collective-permute-start | bytes 196616 | tf_op jit(solution)/shard_map/ppermute | solution.py:413
  29.0 7.8 %collective-permute-start = (bf16[2,128,128]{2,1,0:T(8,128)(2,1)}, bf16[2,128,128]{2,1,0:T(8,128)(2,1)S(1)}, u32[]{:S(2)}, u32[]{:S(2)}) collective-permute-start(bf16[2,128,128]{2,1,0:T(8,128)(2,1)} %get-tuple-element.12.right_ref), channel_id=1, source_target_pairs={{0,8},{8,16},{16,24},{24,32},{32,40},{40,48},{48,56},{56,64},{64,7... | collective-permute-start | bytes 196616 | tf_op jit(solution)/shard_map/ppermute | solution.py:412
  31.3 9.9 %copy-start.1 = (bf16[2,128,128]{2,1,0:T(8,128)(2,1)}, bf16[2,128,128]{2,1,0:T(8,128)(2,1)S(1)}, u32[]{:S(2)}) copy-start(bf16[2,128,128]{2,1,0:T(8,128)(2,1)S(1)} %collective-permute-done.1.xr_any) | copy-start | bytes 196612
  36.8 4.4 %copy-start.2 = (bf16[2,128,128]{2,1,0:T(8,128)(2,1)}, bf16[2,128,128]{2,1,0:T(8,128)(2,1)S(1)}, u32[]{:S(2)}) copy-start(bf16[2,128,128]{2,1,0:T(8,128)(2,1)S(1)} %collective-permute-done.xl_any) | copy-start | bytes 196612
  36.8 4.4 %collective-permute-start.2 = (bf16[8,8,128]{2,1,0:T(8,128)(2,1)S(1)}, bf16[8,8,128]{2,1,0:T(8,128)(2,1)S(1)}, u32[]{:S(2)}, u32[]{:S(2)}) collective-permute-start(bf16[8,8,128]{2,1,0:T(8,128)(2,1)S(1)} %pad_maximum_fusion), channel_id=1, source_target_pairs={{0,1},{1,2},{2,3},{3,4},{4,5},{5,6},{6,7},{7,0},{8,9},{9,10},{10,1... | collective-permute-start | bytes 49160 | tf_op jit(solution)/shard_map/ppermute | solution.py:415
  36.8 4.4 %collective-permute-start.3 = (bf16[8,8,128]{2,1,0:T(8,128)(2,1)S(1)}, bf16[8,8,128]{2,1,0:T(8,128)(2,1)S(1)}, u32[]{:S(2)}, u32[]{:S(2)}) collective-permute-start(bf16[8,8,128]{2,1,0:T(8,128)(2,1)S(1)} %pad_maximum_fusion.1), channel_id=1, source_target_pairs={{1,0},{2,1},{3,2},{4,3},{5,4},{6,5},{7,6},{0,7},{9,8},{10,9},{11,1... | collective-permute-start | bytes 49160 | tf_op jit(solution)/shard_map/ppermute | solution.py:416
  41.2 0.6 copy-start.3
  41.2 0.6 copy-start.4

commit v3 on v2

v3 whole, which is shorter than its diff:
```python
import math

import jax
import jax.numpy as jnp
import numpy as np
from jax import lax
from jax.experimental import pallas as pl
from jax.experimental.pallas import tpu as pltpu
from jax.sharding import PartitionSpec as P

F32 = jnp.float32
BF16 = jnp.bfloat16
I32 = jnp.int32
VMEM = pltpu.VMEM

NT = (((1,), (1,)), ((), ()))
NN = (((1,), (0,)), ((), ()))

N_BY = 8
Y1 = 144
K_TAPS = 9 * 384


def dot(a, b, dims=NN):
    return lax.dot_general(a, b, dims, preferred_element_type=F32)


def leaky(u):
    return jnp.where(u > 0, u, 0.1 * u)


def split2(v):
    high = v.astype(BF16)
    return high, (v - high.astype(F32)).astype(BF16)


def pack_kernel(dest_ref, cell_ref, value_ref, out_ref):
    rows = dest_ref.shape[1]
    step = 256
    brick = lax.broadcasted_iota(I32, (128, step), 0)
    before = (
        lax.broadcasted_iota(I32, (step, step), 0) < lax.broadcasted_iota(I32, (step, step), 1)
    ).astype(F32).astype(BF16)
    slot_ids = lax.broadcasted_iota(I32, (32, step), 0)
    seen = jnp.zeros((128, 1), F32)
    total = jnp.zeros((128, 256), F32)
    for start in range(0, rows, step):
        here = slice(start, start + step)
        hot = (brick == dest_ref[:, here]).astype(F32)
        hot_b = hot.astype(BF16)
        prefix = dot(hot_b, before) + seen
        slot = jnp.sum(hot * prefix, axis=0, keepdims=True).astype(I32)
        seen = prefix[:, step - 1 :] + hot[:, step - 1 :]
        mine = slot_ids == slot
        pieces = [cell_ref[:, here].astype(F32)] + [value_ref[f : f + 1, here] for f in range(3)]
        highs, lows = [], []
        for piece in pieces:
            high = piece.astype(BF16).astype(F32)
            highs.append(jnp.where(mine, high, 0.0))
            lows.append(jnp.where(mine, piece - high, 0.0))
        spread = jnp.concatenate(highs + lows, axis=0).astype(BF16)
        total = total + dot(hot_b, spread, NT)
    table = total[:, :128] + total[:, 128:]
    for k, shifted in enumerate(
        (
            table,
            jnp.concatenate([table[128 - N_BY :], table[: 128 - N_BY]], axis=0),
            jnp.concatenate([table[N_BY:], table[:N_BY]], axis=0),
        )
    ):
        out_ref[:, k, :] = shifted


def pack(dest, cell, values):
    return pl.pallas_call(
        pack_kernel,
        out_shape=jax.ShapeDtypeStruct((128, 3, 128), F32),
        name="pack",
    )(dest, cell, values)


def paint_kernel(in_ref, after_any, out_ref, first_ref, last_ref, acc_ref):
    z_ids = lax.broadcasted_iota(I32, (16, 128), 0)
    blank = jnp.zeros((16, 128), F32)
    group = 8
    for table, base, shift, rows in ((1, 0, 256, 256), (0, 256, 0, 512), (2, 768, 0, 256)):
        turned = jnp.transpose(in_ref[:, table, :], (1, 0))
        cells = turned[0:32].astype(I32)
        place = ((cells >> 8) & 3) * 128 + (cells & 127) - shift
        code = ((cells >> 7) & 1) * 16 + (cells >> 10)
        parts = []
        for f in range(3):
            value = turned[32 + 32 * f : 64 + 32 * f]
            high = value.astype(BF16).astype(F32)
            parts.append((high, value - high))
        place_ids = lax.broadcasted_iota(I32, (rows, 128), 0)
        for start in range(0, 32, group):
            hots, sides = [], []
            for s in range(start, start + group):
                hots.append((place_ids == place[s : s + 1]).astype(F32).astype(BF16))
                column = []
                for part in range(2):
                    for par in range(2):
                        here = z_ids + par * 16 == code[s : s + 1]
                        for f in range(3):
                            column.append(jnp.where(here, parts[f][part][s : s + 1], 0.0))
                        column.append(blank)
                sides.append(jnp.concatenate(column, axis=0).astype(BF16))
            added = dot(jnp.concatenate(hots, axis=1), jnp.concatenate(sides, axis=1), NT)
            if start == 0:
                acc_ref[base : base + rows] = added
            else:
                acc_ref[base : base + rows] += added
    painted = (acc_ref[:, :128] + acc_ref[:, 128:]).reshape(8, 128, 128)
    out_ref[...] = painted.astype(BF16)
    first_ref[...] = painted[:, 0:8].astype(BF16)
    last_ref[...] = painted[:, 120:128].astype(BF16)


def paint(incoming, after):
    edge = jax.ShapeDtypeStruct((8, 8, 128), BF16)
    return pl.pallas_call(
        paint_kernel,
        in_specs=[pl.BlockSpec(memory_space=pltpu.VMEM), pl.BlockSpec(memory_space=pl.ANY)],
        out_shape=(jax.ShapeDtypeStruct((8, 128, 128), BF16), edge, edge),
        scratch_shapes=[VMEM((1024, 256), F32)],
        name="paint",
    )(incoming, after)


def weights_kernel(win_ref, r1_ref):
    lane = lax.broadcasted_iota(I32, (16, 128), 1)
    depth = lax.broadcasted_iota(I32, (16, 128), 0)
    blank = jnp.zeros((16, 128), F32)
    hits = []
    for tile in range(8):
        first_z = 14 + 4 * tile if tile < 4 else 13 + 4 * (tile - 4)
        tap_z = (depth - first_z - 2 * (lane // 64) + 49) % 16
        hits.append([tap_z == tz for tz in range(3)])
    for tx in range(3):
        for ty in range(3):
            rows = [
                [
                    jnp.broadcast_to(
                        jnp.concatenate([win_ref[tx, tz * 3 + f, ty : ty + 1, :].astype(F32)] * 2, axis=1),
                        (16, 128),
                    )
                    for tz in range(3)
                ]
                for f in range(3)
            ]
            for tile in range(8):
                column = []
                for f in range(3):
                    block = blank
                    for tz in range(3):
                        block = jnp.where(hits[tile][tz], rows[f][tz], block)
                    column.append(block)
                block = jnp.concatenate(column + [blank], axis=0).astype(BF16)
                for out in range(2):
                    at = ty * 256 + (tx + out) * 64
                    r1_ref[out * 8 + tile, at : at + 64] = block
    none = jnp.zeros((64, 128), BF16)
    for ty in range(3):
        for tile in range(8):
            r1_ref[tile, ty * 256 + 192 : ty * 256 + 256] = none
            r1_ref[8 + tile, ty * 256 : ty * 256 + 64] = none


def late_weights_kernel(wmid_ref, wout_ref, w2_ref, w3_ref):
    low = lax.broadcasted_iota(I32, (64, 128), 1) < 64
    zero = jnp.zeros((64, 128), F32)
    for source, target, window in ((wmid_ref, w2_ref, (0, 1, 2, 3, 4, 5)), (wout_ref, w3_ref, (0, 1, 3, 2, 4, 5))):
        for tap in range(9):
            front = source[tap // 3, tap % 3, :, 0:128].astype(F32)
            back = jnp.concatenate(
                [source[tap // 3, tap % 3, :, 128:192].astype(F32), jnp.zeros((64, 64), F32)], axis=1
            )
            front = jnp.transpose(jnp.concatenate([front, front], axis=0), (1, 0))
            back = jnp.transpose(jnp.concatenate([back, back], axis=0), (1, 0))
            taps = (front[0:64], front[64:128], back[0:64])
            for at, w in enumerate(window):
                rows = slice(tap * 384 + at * 64, tap * 384 + at * 64 + 64)
                for h in range(2):
                    a = taps[w - 2 * h] if 0 <= w - 2 * h < 3 else zero
                    b = taps[w - 2 * h - 1] if 0 <= w - 2 * h - 1 < 3 else zero
                    natural = jnp.where(low, a, b).astype(BF16)
                    if target is w2_ref:
                        target[h, rows] = jnp.where(low, b, a).astype(BF16)
                        target[2 + h, rows] = natural
                    else:
                        target[h, rows] = natural


def weights(win):
    return pl.pallas_call(
        weights_kernel,
        out_shape=jax.ShapeDtypeStruct((16, 768, 128), BF16),
        name="weights",
    )(win)


def late_weights(wmid, wout):
    return pl.pallas_call(
        late_weights_kernel,
        out_shape=(
            jax.ShapeDtypeStruct((4, K_TAPS, 128), BF16),
            jax.ShapeDtypeStruct((2, K_TAPS, 128), BF16),
        ),
        name="late_weights",
    )(wmid, wout)


def layers_kernel(
    painted_ref, top_ref, bottom_ref, r1_any, w2_any, w3_any, out_any,
    r1_ref, w2_ref, w3_ref, ext_ref, v1_ref, tmp_ref, first_ref, second_ref, rows_ref, third_ref, out_ref,
    in_sem, out_sem,
):
    copies = [
        pltpu.make_async_copy(a, b, in_sem.at[i])
        for i, (a, b) in enumerate(((r1_any, r1_ref), (w2_any, w2_ref), (w3_any, w3_ref)))
    ]
    copies[0].start()
    ext_ref[:, 144:160] = jnp.zeros((8, 16, 128), F32)
    tmp_ref[:, :, Y1:152] = jnp.zeros((2, 7, 8, 128), F32)
    ext_ref[:, 0:8] = top_ref[...].astype(F32)
    ext_ref[:, 136:144] = bottom_ref[...].astype(F32)
    ext_ref[:, 8:136] = painted_ref[...].astype(F32)
    for ty in range(3):
        for pair in range(8):
            v1_ref[ty, pair * Y1 : pair * Y1 + Y1] = ext_ref[pair, 4 + ty : 4 + ty + Y1].astype(BF16)
    copies[0].wait()
    copies[1].start()
    copies[2].start()

    def first_columns(column, carry):
        lhs = jnp.concatenate(
            [v1_ref[ty, p * Y1 : p * Y1 + 7 * Y1] for ty in range(3) for p in range(2)], axis=1
        )
        rhs = jnp.concatenate([r1_ref[2 * column], r1_ref[2 * column + 1]], axis=1)
        u = leaky(dot(lhs, rhs))
        for h in range(2):
            tmp_ref[h, :, 0:Y1] = u[:, h * 128 : h * 128 + 128].reshape(7, Y1, 128)
        out = column // 4
        for h in range(2):
            tile = (column % 4) * 2 + h
            for m in range(7):
                row = pl.multiple_of((2 * m + out) * Y1, Y1)
                for s in range(3):
                    first_ref[s, tile, pl.ds(row, Y1)] = tmp_ref[h, m, 2 * s : 2 * s + Y1].astype(BF16)
        return carry

    lax.fori_loop(0, 8, first_columns, 0)
    copies[1].wait()

    low = lax.broadcasted_iota(I32, (5 * Y1, 128), 1) < 64

    def second_rows(step, carry):
        group = step // 2
        b = step % 2
        outs = []
        for parity in range(2):
            pieces = []
            for tx in range(3):
                row = pl.multiple_of((group * 5 + 2 * tx) * Y1, Y1)
                for ty in range(3):
                    for w in range(3):
                        tile = parity * 4 + (2 * b + w) % 4
                        pieces.append(first_ref[ty, tile, pl.ds(row, 5 * Y1)])
            rhs = jnp.concatenate([w2_ref[2 * parity], w2_ref[2 * parity + 1]], axis=1)
            outs.append(leaky(dot(jnp.concatenate(pieces, axis=1), rhs)))
        even, odd = outs
        for h in range(2):
            e = even[:, h * 128 : h * 128 + 128]
            o = odd[:, h * 128 : h * 128 + 128]
            for k, merged in enumerate((jnp.where(low, o, e), jnp.where(low, e, o))):
                tmp_ref[k, 0:5, 0:Y1] = merged.reshape(5, Y1, 128)
            for k in range(2):
                tile = 4 * b + 2 * h + k
                for q in range(5):
                    row = pl.multiple_of((group * 5 + q) * 128, 128)
                    for s in range(3):
                        second_ref[s, tile, pl.ds(row, 128)] = tmp_ref[k, q, s : s + 128].astype(BF16)
        return carry

    lax.fori_loop(0, 4, second_rows, 0)
    copies[2].wait()

    def third_rows(b):
        pieces = []
        for tx in range(3):
            for ty in range(3):
                for w in range(3):
                    pieces.append(second_ref[ty, (2 * b + w) % 8, tx * 128 : tx * 128 + 1024])
        rhs = jnp.concatenate([w3_ref[0], w3_ref[1]], axis=1)
        u = leaky(dot(jnp.concatenate(pieces, axis=1), rhs))
        for h in range(2):
            rows_ref[b % 2, h] = u[:, h * 128 : h * 128 + 128]

    def third_planes(b):
        for x in range(8):
            for h in range(2):
                turned = jnp.transpose(rows_ref[b % 2, h, x * 128 : x * 128 + 128], (1, 0))
                for k in range(2):
                    third_ref[2 * h + k, pl.ds(x, 64, stride=8), :] = turned[64 * k : 64 * k + 64]
        for j in range(4):
            out_ref[4 * b + j] = third_ref[j].astype(BF16)
        copy = pltpu.make_async_copy(
            out_ref.at[4 * b : 4 * b + 4], out_any.at[4 * b : 4 * b + 4], out_sem.at[b]
        )
        copy.start()
        return copy

    sent = []
    for b in range(4):
        third_rows(b)
        if b:
            sent.append(third_planes(b - 1))
    sent.append(third_planes(3))
    for copy in sent:
        copy.wait()


def layers(painted, top, bottom, r1, w2, w3):
    whole = pl.BlockSpec(memory_space=pltpu.VMEM)
    anywhere = pl.BlockSpec(memory_space=pl.ANY)
    return pl.pallas_call(
        layers_kernel,
        in_specs=[whole] * 3 + [anywhere] * 3,
        out_specs=anywhere,
        out_shape=jax.ShapeDtypeStruct((16, 512, 128), BF16),
        scratch_shapes=[
            VMEM((16, 768, 128), BF16),
            VMEM((4, K_TAPS, 128), BF16),
            VMEM((2, K_TAPS, 128), BF16),
            VMEM((8, 160, 128), F32),
            VMEM((3, 8 * Y1, 128), BF16),
            VMEM((2, 7, 152, 128), F32),
            VMEM((3, 8, 14 * Y1, 128), BF16),
            VMEM((3, 8, 10 * 128, 128), BF16),
            VMEM((2, 2, 1024, 128), F32),
            VMEM((4, 512, 128), F32),
            VMEM((16, 512, 128), BF16),
            pltpu.SemaphoreType.DMA((3,)),
            pltpu.SemaphoreType.DMA((4,)),
        ],
        compiler_params=pltpu.CompilerParams(vmem_limit_bytes=60 << 20),
        name="layers",
    )(painted, top, bottom, r1, w2, w3)


def twiddle_rows(count):
    position = np.arange(count, dtype=np.int64)
    phase = position[:, None] * position[None, :] % count
    angle = phase.astype(np.float32) * np.float32(2.0 * math.pi / count)
    factor = np.float32(1.0 / math.sqrt(count))
    parts = np.stack([np.cos(angle) * factor, -np.sin(angle) * factor])
    parts = parts.reshape(2 * count, count // 8, 8)
    table = np.zeros((2, 2 * count, count // 8, 2, 8), np.float32)
    for parity in range(2):
        table[parity, :, :, parity, :] = parts
    return table.reshape(4 * count, 2, count).transpose(1, 0, 2)


def transform_kernel(twiddle_ref, in_any, out_any, in_ref, out_ref, in_sem, out_sem):
    chunks = 8
    rows = 512 // chunks
    channels = 64 // chunks
    arrivals = []
    for i in range(chunks):
        here = slice(i * rows, i * rows + rows)
        copy = pltpu.make_async_copy(in_any.at[:, here], in_ref.at[:, here], in_sem.at[i])
        copy.start()
        arrivals.append(copy)
    lhs = jnp.concatenate([twiddle_ref[0], twiddle_ref[1]], axis=1)
    sent = []
    for i in range(chunks):
        arrivals[i].wait()
        for pair in range(channels // 4):
            at = i * rows + pair * 32
            rhs = jnp.concatenate(
                [in_ref[:, at + k * 16 : at + k * 16 + 16].reshape(256, 128) for k in range(2)], axis=1
            )
            u = dot(lhs, rhs).astype(BF16)
            for k in range(2):
                for parity in range(2):
                    for t in range(2):
                        row = (parity * 2 + t) * 128
                        out_ref[t, i * channels + 4 * pair + 2 * k + parity, 0] = (
                            u[row : row + 128, k * 128 : k * 128 + 128]
                        )
        here = slice(i * channels, i * channels + channels)
        copy = pltpu.make_async_copy(out_ref.at[:, here], out_any.at[:, here], out_sem.at[i])
        copy.start()
        sent.append(copy)
    for copy in sent:
        copy.wait()


def transform(twiddle, moved):
    anywhere = pl.BlockSpec(memory_space=pl.ANY)
    return pl.pallas_call(
        transform_kernel,
        in_specs=[pl.BlockSpec(memory_space=pltpu.VMEM), anywhere],
        out_specs=anywhere,
        out_shape=jax.ShapeDtypeStruct((2, 64, 1, 128, 128), BF16),
        scratch_shapes=[
            VMEM((16, 512, 128), BF16),
            VMEM((2, 64, 1, 128, 128), BF16),
            pltpu.SemaphoreType.DMA((8,)),
            pltpu.SemaphoreType.DMA((8,)),
        ],
        name="transform",
    )(twiddle, moved)


def on_device(particle_values, destination, cell_index, weight_in, weight_mid, weight_out):
    count_x = lax.axis_size("bx")
    count_y = lax.axis_size("by")
    up_y = [(i, (i + 1) % count_y) for i in range(count_y)]
    down_y = [((i + 1) % count_y, i) for i in range(count_y)]

    outgoing = pack(destination.reshape(1, -1), cell_index.reshape(1, -1), particle_values)
    incoming = lax.all_to_all(outgoing, ("bx", "by"), split_axis=0, concat_axis=0, tiled=True)

    r1 = weights(jnp.transpose(weight_in, (0, 3, 1, 2)))
    painted, first_y, last_y = paint(incoming, r1)
    top = lax.ppermute(last_y, "by", up_y)
    bottom = lax.ppermute(first_y, "by", down_y)
    w2, w3 = late_weights(weight_mid, weight_out)
    third = layers(painted, top, bottom, r1, w2, w3)
    moved = lax.all_to_all(third, "bx", split_axis=0, concat_axis=0, tiled=True)
    twiddle = jnp.asarray(twiddle_rows(count_x * 8), BF16)
    return transform(twiddle, moved)


def solution(mesh):
    placed = (P(None, ("bx", "by")), P(("bx", "by"), None), P(("bx", "by")), P(), P(), P())
    return jax.shard_map(
        on_device,
        mesh=mesh,
        in_specs=placed,
        out_specs=P(None, None, "bx", None, "by"),
        check_vma=False,
    )
```

time: 112 us -> 105 us (0.938)
  waiting for transfers between devices: 13.4 us -> 7.78 us
  Pallas kernels: 46.6 us -> 50.7 us
  blocking collectives: 33.2 us -> 30.8 us
  starting transfers between devices: 16.2 us -> 14.1 us
    ppermute x4 -> x2, waiting for transfers between devices: 8.6 us -> 0.01 us  [the longest x1 0.01 us: on_device(): top = lax.ppermute(last_y, 'by', up_y)]
    pallas_call x5 -> x6, Pallas kernels: 46.6 us -> 50.7 us  [the longest x1 31.3 us: layers(): pl.pallas_call(layers_kernel, in_specs=[whole] * 3 + [anywhere] * 3, out_...]
    all_to_all x1, waiting for transfers between devices: 4.82 us -> 7.78 us  [on_device(): lax.all_to_all(outgoing, ('bx', 'by'), split_axis=0, concat_axis=0, tiled...]
    all_to_all x1, blocking collectives: 33.2 us -> 30.8 us  [on_device(): moved = lax.all_to_all(third, 'bx', split_axis=0, concat_axis=0, tiled=True)]
    ppermute x4 -> x2, starting transfers between devices: 5.05 us -> 2.96 us  [the longest x1 2.95 us: on_device(): bottom = lax.ppermute(first_y, 'by', down_y)]
  transfers between devices with their start and end apart: 5 -> 3, of which waited for: 4 -> 1; matrix products, arithmetic and copies ran while one was open for 1% -> 0% of each run, Pallas kernels for 4% -> 7%
where the time goes in v3:
time: 105 us
  Pallas kernels  50.7 us (48%)
  blocking collectives  30.8 us (29%)
  starting transfers between devices  14.1 us (13%)
  waiting for transfers between devices  7.78 us (7%)
  local copies, waits for them, and re-layouts  1.3 us (1%)
    pallas_call x1, Pallas kernels, layers(): pl.pallas_call(layers_kernel, in_specs=[whole] * 3 + [anywhere] * 3, out_...  31.3 us
    all_to_all x1, blocking collectives, on_device(): moved = lax.all_to_all(third, 'bx', split_axis=0, concat_axis=0, tiled=True)  30.8 us
    all_to_all x1, starting transfers between devices, on_device(): lax.all_to_all(outgoing, ('bx', 'by'), split_axis=0, concat_axis=0, tiled...  11.2 us
    all_to_all x1, waiting for transfers between devices, on_device(): lax.all_to_all(outgoing, ('bx', 'by'), split_axis=0, concat_axis=0, tiled...  7.78 us
    pallas_call x1, Pallas kernels, transform(): pl.pallas_call(transform_kernel, in_specs=[pl.BlockSpec(memory_space=pltp...  5.24 us
    pallas_call x1, Pallas kernels, paint(): pl.pallas_call(paint_kernel, in_specs=[pl.BlockSpec(memory_space=pltpu.VM...  4.21 us
    pallas_call x1, Pallas kernels, late_weights(): pl.pallas_call(late_weights_kernel, out_shape=(jax.ShapeDtypeStruct((4, K...  4.06 us
    pallas_call x1, Pallas kernels, weights(): pl.pallas_call(weights_kernel, out_shape=jax.ShapeDtypeStruct((16, 768, 1...  3.15 us
  transfers between devices with their start and end apart: 3, of which 1 were waited for; matrix products, arithmetic and copies ran while one was open for 0% of the time, Pallas kernels for 7%

profile of v3, /device:TPU:0, one launch (start us, length us, event | category | flops | bytes accessed | tf_op | source)
XLA Modules:
  0.0 104.8 jit_solution(17837461099175409806)
XLA Ops:
  0.0 2.8 %pack.1 = f32[128,3,128]{2,1,0:T(4,128)} custom-call(s32[1,2048]{1,0:T(1,128)} %bitcast.4, s32[1,2048]{1,0:T(1,128)} %bitcast.5, f32[3,2048]{1,0:T(4,128)} %value_ref.1), custom_call_target="tpu_custom_call" | custom-call | tf_op jit(solution)/shard_map/pack/pallas_call | solution.py:75
  2.8 11.2 %all-to-all-start = ((f32[128,3,128]{2,1,0:T(4,128)}), f32[128,3,128]{2,1,0:T(4,128)S(1)}, u32[]{:S(2)}, u32[]{:S(2)}) async-start(f32[128,3,128]{2,1,0:T(4,128)} %pack.1), calls=%async_computation | async-start | bytes 524288 | tf_op jit(solution)/shard_map/all_to_all | solution.py:424
  13.9 3.1 %weights.1.after_any.r1_any = bf16[16,768,128]{2,1,0:T(8,128)(2,1)} custom-call(bf16[3,9,3,64]{3,2,1,0:T(4,128)(2,1)} %bitcast.3), custom_call_target="tpu_custom_call" | custom-call | tf_op jit(solution)/shard_map/weights/pallas_call | solution.py:196
  17.1 7.8 %all-to-all-done.in_ref = f32[128,3,128]{2,1,0:T(4,128)S(1)} async-done(((f32[128,3,128]{2,1,0:T(4,128)}), f32[128,3,128]{2,1,0:T(4,128)S(1)}, u32[]{:S(2)}, u32[]{:S(2)}) %all-to-all-start) | async-done | bytes 196640 | tf_op jit(solution)/shard_map/all_to_all | solution.py:424
  24.9 0.0 copy-start
  24.9 0.7 copy-done
  25.6 4.2 %paint.1 = (bf16[8,128,128]{2,1,0:T(8,128)(2,1)}, bf16[8,8,128]{2,1,0:T(8,128)(2,1)}, bf16[8,8,128]{2,1,0:T(8,128)(2,1)}) custom-call(f32[128,3,128]{2,1,0:T(4,128)} %copy-done, bf16[16,768,128]{2,1,0:T(8,128)(2,1)} %weights.1.after_any.r1_any), custom_call_target="tpu_custom_call" | custom-call | tf_op jit(solution)/shard_map/paint/pallas_call | solution.py:122
  29.8 0.0 collective-permute-start
  29.8 3.0 %collective-permute-start.1 = (bf16[8,8,128]{2,1,0:T(8,128)(2,1)}, bf16[8,8,128]{2,1,0:T(8,128)(2,1)S(1)}, u32[]{:S(2)}, u32[]{:S(2)}) collective-permute-start(bf16[8,8,128]{2,1,0:T(8,128)(2,1)} %get-tuple-element.12), channel_id=1, source_target_pairs={{1,0},{2,1},{3,2},{4,3},{5,4},{6,5},{7,6},{0,7},{9,8},{10,9},{11,1... | collective-permute-start | bytes 49160 | tf_op jit(solution)/shard_map/ppermute | solution.py:429
  32.7 4.1 %late_weights.1 = (bf16[4,3456,128]{2,1,0:T(8,128)(2,1)}, bf16[2,3456,128]{2,1,0:T(8,128)(2,1)}) custom-call(bf16[3,3,64,192]{3,2,1,0:T(8,128)(2,1)} %wmid_ref.1, bf16[3,3,64,192]{3,2,1,0:T(8,128)(2,1)} %wout_ref.1), custom_call_target="tpu_custom_call" | custom-call | tf_op jit(solution)/shard_map/late_weights/pallas_call | solution.py:204
  36.8 0.0 collective-permute-done.top_ref
  36.8 0.0 copy-start.1
  36.8 0.0 collective-permute-done.1.bottom_ref
  36.8 0.0 copy-start.2
  36.8 0.6 copy-done.1
  37.4 0.0 copy-done.2
  37.4 31.3 %layers.1 = bf16[16,512,128]{2,1,0:T(8,128)(2,1)} custom-call(bf16[8,128,128]{2,1,0:T(8,128)(2,1)} %get-tuple-element.10.painted_ref, bf16[8,8,128]{2,1,0:T(8,128)(2,1)} %copy-done.1, bf16[8,8,128]{2,1,0:T(8,128)(2,1)} %copy-done.2, bf16[16,768,128]{2,1,0:T(8,128)(2,1)} %weights.1.after_any.r1_any, bf16[4,3456,128]{2,1,0:T(8,128)(2,1)} %get-tuple-element.13.w2_any, ...), custom_call_target="tpu_custom_call" | custom-call | tf_op jit(solution)/shard_map/layers/pallas_call | solution.py:327
  68.7 30.8 %all_to_all.10.in_any = bf16[16,512,128]{2,1,0:T(8,128)(2,1)} all-to-all(bf16[16,512,128]{2,1,0:T(8,128)(2,1)} %layers.1), channel_id=1, replica_groups=mesh['bx'=16,'by'=8] {'bx'}, dimensions={0} | all-to-all | bytes 4194304 | tf_op jit(solution)/shard_map/all_to_all | solution.py:432
  99.5 5.2 %transform.1 = bf16[2,64,1,128,128]{4,3,2,1,0:T(8,128)(2,1)} custom-call(bf16[2,512,128]{2,1,0:T(8,128)(2,1)} %constant.2.clone.twiddle_ref, bf16[16,512,128]{2,1,0:T(8,128)(2,1)} %all_to_all.10.in_any), custom_call_target="tpu_custom_call" | custom-call | tf_op jit(solution)/shard_map/transform/pallas_call | solution.py:402
Async XLA Ops:
  2.8 22.1 %all-to-all-start = ((f32[128,3,128]{2,1,0:T(4,128)}), f32[128,3,128]{2,1,0:T(4,128)S(1)}, u32[]{:S(2)}, u32[]{:S(2)}) async-start(f32[128,3,128]{2,1,0:T(4,128)} %pack.1), calls=%async_computation | async-start | bytes 524288 | tf_op jit(solution)/shard_map/all_to_all | solution.py:424
  24.9 0.7 copy-start
  29.8 7.0 %collective-permute-start = (bf16[8,8,128]{2,1,0:T(8,128)(2,1)}, bf16[8,8,128]{2,1,0:T(8,128)(2,1)S(1)}, u32[]{:S(2)}, u32[]{:S(2)}) collective-permute-start(bf16[8,8,128]{2,1,0:T(8,128)(2,1)} %get-tuple-element.11), channel_id=1, source_target_pairs={{0,1},{1,2},{2,3},{3,4},{4,5},{5,6},{6,7},{7,0},{8,9},{9,10},{10,1... | collective-permute-start | bytes 49160 | tf_op jit(solution)/shard_map/ppermute | solution.py:428
  29.8 7.0 %collective-permute-start.1 = (bf16[8,8,128]{2,1,0:T(8,128)(2,1)}, bf16[8,8,128]{2,1,0:T(8,128)(2,1)S(1)}, u32[]{:S(2)}, u32[]{:S(2)}) collective-permute-start(bf16[8,8,128]{2,1,0:T(8,128)(2,1)} %get-tuple-element.12), channel_id=1, source_target_pairs={{1,0},{2,1},{3,2},{4,3},{5,4},{6,5},{7,6},{0,7},{9,8},{10,9},{11,1... | collective-permute-start | bytes 49160 | tf_op jit(solution)/shard_map/ppermute | solution.py:429
  36.8 0.6 copy-start.1
  36.8 0.6 copy-start.2

commit v4 on v3

--- a/solution.py
+++ b/solution.py
@@ -80,32 +80,58 @@
 
 
 def paint_kernel(in_ref, after_any, out_ref, first_ref, last_ref, acc_ref):
-    z_ids = lax.broadcasted_iota(I32, (16, 128), 0)
-    blank = jnp.zeros((16, 128), F32)
+    z_ids = lax.broadcasted_iota(I32, (16, 128), 0).astype(F32).astype(BF16)
+    y_ids = lax.broadcasted_iota(I32, (128, 128), 0).astype(F32).astype(BF16)
+    one = jnp.ones((16, 128), BF16)
+    blank = jnp.zeros((16, 128), BF16)
     group = 8
-    for table, base, shift, rows in ((1, 0, 256, 256), (0, 256, 0, 512), (2, 768, 0, 256)):
+
+    def spread(row):
+        return jnp.broadcast_to(row, (16, 128)).astype(BF16)
+
+    for table, base, pairs in ((1, 0, (2, 3)), (0, 256, (0, 1, 2, 3)), (2, 768, (0, 1))):
         turned = jnp.transpose(in_ref[:, table, :], (1, 0))
         cells = turned[0:32].astype(I32)
-        place = ((cells >> 8) & 3) * 128 + (cells & 127) - shift
-        code = ((cells >> 7) & 1) * 16 + (cells >> 10)
+        pair = ((cells >> 8) & 3).astype(F32)
+        y = (cells & 127).astype(F32)
+        code = (((cells >> 7) & 1) * 16 + (cells >> 10)).astype(F32)
         parts = []
         for f in range(3):
             value = turned[32 + 32 * f : 64 + 32 * f]
             high = value.astype(BF16).astype(F32)
             parts.append((high, value - high))
-        place_ids = lax.broadcasted_iota(I32, (rows, 128), 0)
+        rows = 128 * len(pairs)
         for start in range(0, 32, group):
             hots, sides = [], []
             for s in range(start, start + group):
-                hots.append((place_ids == place[s : s + 1]).astype(F32).astype(BF16))
+                along_y = jnp.where(
+                    y_ids == jnp.concatenate([spread(y[s : s + 1])] * 8, axis=0),
+                    jnp.concatenate([one] * 8, axis=0),
+                    jnp.concatenate([blank] * 8, axis=0),
+                )
+                my_pair = spread(pair[s : s + 1])
+                hots.append(
+                    jnp.concatenate(
+                        [
+                            along_y
+                            * jnp.concatenate(
+                                [jnp.where(my_pair == jnp.full((16, 128), p, BF16), one, blank)] * 8, axis=0
+                            )
+                            for p in pairs
+                        ],
+                        axis=0,
+                    )
+                )
+                my_code = spread(code[s : s + 1])
                 column = []
                 for part in range(2):
+                    values = [spread(parts[f][part][s : s + 1]) for f in range(3)]
                     for par in range(2):
-                        here = z_ids + par * 16 == code[s : s + 1]
+                        here = z_ids + jnp.full((16, 128), par * 16, BF16) == my_code
                         for f in range(3):
-                            column.append(jnp.where(here, parts[f][part][s : s + 1], 0.0))
+                            column.append(jnp.where(here, values[f], blank))
                         column.append(blank)
-                sides.append(jnp.concatenate(column, axis=0).astype(BF16))
+                sides.append(jnp.concatenate(column, axis=0))
             added = dot(jnp.concatenate(hots, axis=1), jnp.concatenate(sides, axis=1), NT)
             if start == 0:
                 acc_ref[base : base + rows] = added
@@ -128,7 +154,7 @@
     )(incoming, after)
 
 
-def weights_kernel(win_ref, r1_ref):
+def weights_kernel(win_ref, wmid_ref, r1_ref, w2_ref):
     lane = lax.broadcasted_iota(I32, (16, 128), 1)
     depth = lax.broadcasted_iota(I32, (16, 128), 0)
     blank = jnp.zeros((16, 128), F32)
@@ -165,62 +191,57 @@
         for tile in range(8):
             r1_ref[tile, ty * 256 + 192 : ty * 256 + 256] = none
             r1_ref[8 + tile, ty * 256 : ty * 256 + 64] = none
-
-
-def late_weights_kernel(wmid_ref, wout_ref, w2_ref, w3_ref):
+    tap_rows(wmid_ref, w2_ref, (0, 1, 2, 3, 4, 5), True)
+
+
+def tap_rows(source, target, window, swapped):
     low = lax.broadcasted_iota(I32, (64, 128), 1) < 64
     zero = jnp.zeros((64, 128), F32)
-    for source, target, window in ((wmid_ref, w2_ref, (0, 1, 2, 3, 4, 5)), (wout_ref, w3_ref, (0, 1, 3, 2, 4, 5))):
-        for tap in range(9):
-            front = source[tap // 3, tap % 3, :, 0:128].astype(F32)
-            back = jnp.concatenate(
-                [source[tap // 3, tap % 3, :, 128:192].astype(F32), jnp.zeros((64, 64), F32)], axis=1
-            )
-            front = jnp.transpose(jnp.concatenate([front, front], axis=0), (1, 0))
-            back = jnp.transpose(jnp.concatenate([back, back], axis=0), (1, 0))
-            taps = (front[0:64], front[64:128], back[0:64])
-            for at, w in enumerate(window):
-                rows = slice(tap * 384 + at * 64, tap * 384 + at * 64 + 64)
-                for h in range(2):
-                    a = taps[w - 2 * h] if 0 <= w - 2 * h < 3 else zero
-                    b = taps[w - 2 * h - 1] if 0 <= w - 2 * h - 1 < 3 else zero
-                    natural = jnp.where(low, a, b).astype(BF16)
-                    if target is w2_ref:
-                        target[h, rows] = jnp.where(low, b, a).astype(BF16)
-                        target[2 + h, rows] = natural
-                    else:
-                        target[h, rows] = natural
-
-
-def weights(win):
+    for tap in range(9):
+        front = source[tap // 3, tap % 3, :, 0:128].astype(F32)
+        back = jnp.concatenate(
+            [source[tap // 3, tap % 3, :, 128:192].astype(F32), jnp.zeros((64, 64), F32)], axis=1
+        )
+        front = jnp.transpose(jnp.concatenate([front, front], axis=0), (1, 0))
+        back = jnp.transpose(jnp.concatenate([back, back], axis=0), (1, 0))
+        taps = (front[0:64], front[64:128], back[0:64])
+        for at, w in enumerate(window):
+            rows = slice(tap * 384 + at * 64, tap * 384 + at * 64 + 64)
+            for h in range(2):
+                a = taps[w - 2 * h] if 0 <= w - 2 * h < 3 else zero
+                b = taps[w - 2 * h - 1] if 0 <= w - 2 * h - 1 < 3 else zero
+                if swapped:
+                    target[2 + h, rows] = jnp.where(low, b, a).astype(BF16)
+                target[h, rows] = jnp.where(low, a, b).astype(BF16)
+
+
+def late_weights_kernel(wout_ref, w3_ref):
+    tap_rows(wout_ref, w3_ref, (0, 1, 3, 2, 4, 5), False)
+
+
+def weights(win, wmid):
     return pl.pallas_call(
         weights_kernel,
-        out_shape=jax.ShapeDtypeStruct((16, 768, 128), BF16),
+        out_shape=(
+            jax.ShapeDtypeStruct((16, 768, 128), BF16),
+            jax.ShapeDtypeStruct((4, K_TAPS, 128), BF16),
+        ),
         name="weights",
-    )(win)
-
-
-def late_weights(wmid, wout):
+    )(win, wmid)
+
+
+def late_weights(wout):
     return pl.pallas_call(
         late_weights_kernel,
-        out_shape=(
-            jax.ShapeDtypeStruct((4, K_TAPS, 128), BF16),
-            jax.ShapeDtypeStruct((2, K_TAPS, 128), BF16),
-        ),
+        out_shape=jax.ShapeDtypeStruct((2, K_TAPS, 128), BF16),
         name="late_weights",
-    )(wmid, wout)
+    )(wout)
 
 
 def layers_kernel(
-    painted_ref, top_ref, bottom_ref, r1_any, w2_any, w3_any, out_any,
-    r1_ref, w2_ref, w3_ref, ext_ref, v1_ref, tmp_ref, first_ref, second_ref, rows_ref, third_ref, out_ref,
-    in_sem, out_sem,
+    painted_ref, top_ref, bottom_ref, r1_ref, w2_ref, w3_ref, out_any,
+    ext_ref, v1_ref, tmp_ref, first_ref, second_ref, rows_ref, third_ref, out_ref, out_sem,
 ):
-    copies = [
-        pltpu.make_async_copy(a, b, in_sem.at[i])
-        for i, (a, b) in enumerate(((r1_any, r1_ref), (w2_any, w2_ref), (w3_any, w3_ref)))
-    ]
-    copies[0].start()
     ext_ref[:, 144:160] = jnp.zeros((8, 16, 128), F32)
     tmp_ref[:, :, Y1:152] = jnp.zeros((2, 7, 8, 128), F32)
     ext_ref[:, 0:8] = top_ref[...].astype(F32)
@@ -229,9 +250,6 @@
     for ty in range(3):
         for pair in range(8):
             v1_ref[ty, pair * Y1 : pair * Y1 + Y1] = ext_ref[pair, 4 + ty : 4 + ty + Y1].astype(BF16)
-    copies[0].wait()
-    copies[1].start()
-    copies[2].start()
 
     def first_columns(column, carry):
         lhs = jnp.concatenate(
@@ -251,7 +269,6 @@
         return carry
 
     lax.fori_loop(0, 8, first_columns, 0)
-    copies[1].wait()
 
     low = lax.broadcasted_iota(I32, (5 * Y1, 128), 1) < 64
 
@@ -267,7 +284,7 @@
                     for w in range(3):
                         tile = parity * 4 + (2 * b + w) % 4
                         pieces.append(first_ref[ty, tile, pl.ds(row, 5 * Y1)])
-            rhs = jnp.concatenate([w2_ref[2 * parity], w2_ref[2 * parity + 1]], axis=1)
+            rhs = jnp.concatenate([w2_ref[2 - 2 * parity], w2_ref[3 - 2 * parity]], axis=1)
             outs.append(leaky(dot(jnp.concatenate(pieces, axis=1), rhs)))
         even, odd = outs
         for h in range(2):
@@ -284,7 +301,6 @@
         return carry
 
     lax.fori_loop(0, 4, second_rows, 0)
-    copies[2].wait()
 
     def third_rows(b):
         pieces = []
@@ -326,13 +342,10 @@
     anywhere = pl.BlockSpec(memory_space=pl.ANY)
     return pl.pallas_call(
         layers_kernel,
-        in_specs=[whole] * 3 + [anywhere] * 3,
+        in_specs=[whole] * 6,
         out_specs=anywhere,
         out_shape=jax.ShapeDtypeStruct((16, 512, 128), BF16),
         scratch_shapes=[
-            VMEM((16, 768, 128), BF16),
-            VMEM((4, K_TAPS, 128), BF16),
-            VMEM((2, K_TAPS, 128), BF16),
             VMEM((8, 160, 128), F32),
             VMEM((3, 8 * Y1, 128), BF16),
             VMEM((2, 7, 152, 128), F32),
@@ -341,10 +354,9 @@
             VMEM((2, 2, 1024, 128), F32),
             VMEM((4, 512, 128), F32),
             VMEM((16, 512, 128), BF16),
-            pltpu.SemaphoreType.DMA((3,)),
             pltpu.SemaphoreType.DMA((4,)),
         ],
-        compiler_params=pltpu.CompilerParams(vmem_limit_bytes=60 << 20),
+        compiler_params=pltpu.CompilerParams(vmem_limit_bytes=44 << 20),
         name="layers",
     )(painted, top, bottom, r1, w2, w3)
 
@@ -362,56 +374,41 @@
     return table.reshape(4 * count, 2, count).transpose(1, 0, 2)
 
 
-def transform_kernel(twiddle_ref, in_any, out_any, in_ref, out_ref, in_sem, out_sem):
-    chunks = 8
-    rows = 512 // chunks
-    channels = 64 // chunks
-    arrivals = []
-    for i in range(chunks):
-        here = slice(i * rows, i * rows + rows)
-        copy = pltpu.make_async_copy(in_any.at[:, here], in_ref.at[:, here], in_sem.at[i])
-        copy.start()
-        arrivals.append(copy)
+def transform_kernel(twiddle_ref, in_ref, out_ref):
     lhs = jnp.concatenate([twiddle_ref[0], twiddle_ref[1]], axis=1)
-    sent = []
-    for i in range(chunks):
-        arrivals[i].wait()
-        for pair in range(channels // 4):
-            at = i * rows + pair * 32
-            rhs = jnp.concatenate(
-                [in_ref[:, at + k * 16 : at + k * 16 + 16].reshape(256, 128) for k in range(2)], axis=1
-            )
-            u = dot(lhs, rhs).astype(BF16)
-            for k in range(2):
-                for parity in range(2):
-                    for t in range(2):
-                        row = (parity * 2 + t) * 128
-                        out_ref[t, i * channels + 4 * pair + 2 * k + parity, 0] = (
-                            u[row : row + 128, k * 128 : k * 128 + 128]
-                        )
-        here = slice(i * channels, i * channels + channels)
-        copy = pltpu.make_async_copy(out_ref.at[:, here], out_any.at[:, here], out_sem.at[i])
-        copy.start()
-        sent.append(copy)
-    for copy in sent:
-        copy.wait()
+    base = pl.multiple_of(pl.program_id(0) * 256, 256)
+    for pair in range(8):
+        rhs = jnp.concatenate(
+            [
+                in_ref[:, pl.ds(base + (2 * pair + k) * 16, 16)].reshape(256, 128)
+                for k in range(2)
+            ],
+            axis=1,
+        )
+        u = dot(lhs, rhs).astype(BF16)
+        for k in range(2):
+            for parity in range(2):
+                for t in range(2):
+                    at = (parity * 2 + t) * 128
+                    out_ref[t, 4 * pair + 2 * k + parity, 0] = u[at : at + 128, k * 128 : k * 128 + 128]
 
 
 def transform(twiddle, moved):
-    anywhere = pl.BlockSpec(memory_space=pl.ANY)
     return pl.pallas_call(
         transform_kernel,
-        in_specs=[pl.BlockSpec(memory_space=pltpu.VMEM), anywhere],
-        out_specs=anywhere,
+        grid=(2,),
+        in_specs=[
+            pl.BlockSpec((2, 512, 128), lambda i: (0, 0, 0)),
+            pl.BlockSpec(memory_space=pltpu.VMEM),
+        ],
+        out_specs=pl.BlockSpec((2, 32, 1, 128, 128), lambda i: (0, i, 0, 0, 0)),
         out_shape=jax.ShapeDtypeStruct((2, 64, 1, 128, 128), BF16),
-        scratch_shapes=[
-            VMEM((16, 512, 128), BF16),
-            VMEM((2, 64, 1, 128, 128), BF16),
-            pltpu.SemaphoreType.DMA((8,)),
-            pltpu.SemaphoreType.DMA((8,)),
-        ],
         name="transform",
     )(twiddle, moved)
+
+
+def in_vmem(value):
+    return pltpu.with_memory_space_constraint(value, pltpu.VMEM)
 
 
 def on_device(particle_values, destination, cell_index, weight_in, weight_mid, weight_out):
@@ -423,15 +420,16 @@
     outgoing = pack(destination.reshape(1, -1), cell_index.reshape(1, -1), particle_values)
     incoming = lax.all_to_all(outgoing, ("bx", "by"), split_axis=0, concat_axis=0, tiled=True)
 
-    r1 = weights(jnp.transpose(weight_in, (0, 3, 1, 2)))
+    r1, w2 = weights(jnp.transpose(weight_in, (0, 3, 1, 2)), weight_mid)
+    incoming = in_vmem(incoming)
     painted, first_y, last_y = paint(incoming, r1)
     top = lax.ppermute(last_y, "by", up_y)
     bottom = lax.ppermute(first_y, "by", down_y)
-    w2, w3 = late_weights(weight_mid, weight_out)
-    third = layers(painted, top, bottom, r1, w2, w3)
+    w3 = late_weights(weight_out)
+    third = layers(*(in_vmem(v) for v in (painted, top, bottom, r1, w2, w3)))
     moved = lax.all_to_all(third, "bx", split_axis=0, concat_axis=0, tiled=True)
     twiddle = jnp.asarray(twiddle_rows(count_x * 8), BF16)
-    return transform(twiddle, moved)
+    return transform(twiddle, in_vmem(moved))
 
 
 def solution(mesh):

time: 105 us -> 101 us (0.962)
  Pallas kernels: 50.7 us -> 45.7 us
  local copies, waits for them, and re-layouts: 1.3 us -> 4.42 us
  waiting for transfers between devices: 7.78 us -> 6.03 us
    pallas_call x4, Pallas kernels: 43.8 us -> 39.7 us  [the longest x1 28.5 us: layers(): pl.pallas_call(layers_kernel, in_specs=[whole] * 6, out_specs=anywhere, o...]
    unnamed x6 -> x8, local copies, waits for them, and re-layouts: 1.3 us -> 4.42 us
    all_to_all x1, waiting for transfers between devices: 7.78 us -> 6.02 us  [on_device(): lax.all_to_all(outgoing, ('bx', 'by'), split_axis=0, concat_axis=0, tiled...]
where the time goes in v4:
time: 101 us
  Pallas kernels  45.7 us (45%)
  blocking collectives  30.5 us (30%)
  starting transfers between devices  14.1 us (14%)
  waiting for transfers between devices  6.03 us (6%)
  local copies, waits for them, and re-layouts  4.42 us (4%)
    all_to_all x1, blocking collectives, on_device(): moved = lax.all_to_all(third, 'bx', split_axis=0, concat_axis=0, tiled=True)  30.5 us
    pallas_call x1, Pallas kernels, layers(): pl.pallas_call(layers_kernel, in_specs=[whole] * 6, out_specs=anywhere, o...  28.5 us
    all_to_all x1, starting transfers between devices, on_device(): lax.all_to_all(outgoing, ('bx', 'by'), split_axis=0, concat_axis=0, tiled...  11.2 us
    all_to_all x1, waiting for transfers between devices, on_device(): lax.all_to_all(outgoing, ('bx', 'by'), split_axis=0, concat_axis=0, tiled...  6.02 us
    pallas_call x1, Pallas kernels, weights(): pl.pallas_call(weights_kernel, out_shape=(jax.ShapeDtypeStruct((16, 768,...  4.9 us
    unnamed x8, local copies, waits for them, and re-layouts  4.42 us
    pallas_call x1, Pallas kernels, transform(): pl.pallas_call(transform_kernel, grid=(2,), in_specs=[pl.BlockSpec((2, 51...  3.74 us
    pallas_call x1, Pallas kernels, paint(): pl.pallas_call(paint_kernel, in_specs=[pl.BlockSpec(memory_space=pltpu.VM...  3.24 us
  transfers between devices with their start and end apart: 3, of which 1 were waited for; matrix products, arithmetic and copies ran while one was open for 0% of the time, Pallas kernels for 7%

profile of v4, /device:TPU:0, one launch (start us, length us, event | category | flops | bytes accessed | tf_op | source)
XLA Modules:
  0.0 100.8 jit_solution(4208891554688963551)
XLA Ops:
  0.0 2.8 %pack.1 = f32[128,3,128]{2,1,0:T(4,128)} custom-call(s32[1,2048]{1,0:T(1,128)} %bitcast.4, s32[1,2048]{1,0:T(1,128)} %bitcast.5, f32[3,2048]{1,0:T(4,128)} %value_ref.1), custom_call_target="tpu_custom_call" | custom-call | tf_op jit(solution)/shard_map/pack/pallas_call | solution.py:75
  2.8 11.2 %all-to-all-start = ((f32[128,3,128]{2,1,0:T(4,128)}), f32[128,3,128]{2,1,0:T(4,128)S(1)}, u32[]{:S(2)}, u32[]{:S(2)}) async-start(f32[128,3,128]{2,1,0:T(4,128)} %pack.1), calls=%async_computation | async-start | bytes 524288 | tf_op jit(solution)/shard_map/all_to_all | solution.py:421
  13.9 4.9 %weights.1 = (bf16[16,768,128]{2,1,0:T(8,128)(2,1)}, bf16[4,3456,128]{2,1,0:T(8,128)(2,1)}) custom-call(bf16[3,9,3,64]{3,2,1,0:T(4,128)(2,1)} %bitcast.3, bf16[3,3,64,192]{3,2,1,0:T(8,128)(2,1)} %wmid_ref.1), custom_call_target="tpu_custom_call" | custom-call | tf_op jit(solution)/shard_map/weights/pallas_call | solution.py:223
  18.8 0.0 copy-start
  18.8 6.0 %all-to-all-done.in_ref = f32[128,3,128]{2,1,0:T(4,128)S(1)} async-done(((f32[128,3,128]{2,1,0:T(4,128)}), f32[128,3,128]{2,1,0:T(4,128)S(1)}, u32[]{:S(2)}, u32[]{:S(2)}) %all-to-all-start) | async-done | bytes 196640 | tf_op jit(solution)/shard_map/all_to_all | solution.py:421
  24.9 3.2 %paint.1 = (bf16[8,128,128]{2,1,0:T(8,128)(2,1)}, bf16[8,8,128]{2,1,0:T(8,128)(2,1)}, bf16[8,8,128]{2,1,0:T(8,128)(2,1)}) custom-call(f32[128,3,128]{2,1,0:T(4,128)S(1)} %all-to-all-done.in_ref, bf16[16,768,128]{2,1,0:T(8,128)(2,1)} %get-tuple-element.10.after_any.r1_ref), custom_call_target="tpu_custom_call" | custom-call | tf_op jit(solution)/shard_map/paint/pallas_call | solution.py:148
  28.1 0.0 collective-permute-start
  28.1 3.0 %collective-permute-start.1 = (bf16[8,8,128]{2,1,0:T(8,128)(2,1)}, bf16[8,8,128]{2,1,0:T(8,128)(2,1)S(1)}, u32[]{:S(2)}, u32[]{:S(2)}) collective-permute-start(bf16[8,8,128]{2,1,0:T(8,128)(2,1)} %get-tuple-element.13), channel_id=1, source_target_pairs={{1,0},{2,1},{3,2},{4,3},{5,4},{6,5},{7,6},{0,7},{9,8},{10,9},{11,1... | collective-permute-start | bytes 49160 | tf_op jit(solution)/shard_map/ppermute | solution.py:427
  31.1 2.5 %late_weights.1.w3_ref = bf16[2,3456,128]{2,1,0:T(8,128)(2,1)} custom-call(bf16[3,3,64,192]{3,2,1,0:T(8,128)(2,1)} %wout_ref.1), custom_call_target="tpu_custom_call" | custom-call | tf_op jit(solution)/shard_map/late_weights/pallas_call | solution.py:234
  33.6 0.0 collective-permute-done.top_ref
  33.6 0.0 collective-permute-done.1.bottom_ref
  33.6 0.0 copy-done
  33.6 0.0 copy-start.1
  33.6 1.5 %copy-done.1 = bf16[2,3456,128]{2,1,0:T(8,128)(2,1)S(1)} copy-done((bf16[2,3456,128]{2,1,0:T(8,128)(2,1)S(1)}, bf16[2,3456,128]{2,1,0:T(8,128)(2,1)}, u32[]{:S(2)}) %copy-start.1) | copy-done | bytes 1769496
  35.0 0.0 copy-start.2
  35.0 2.0 %copy-done.2 = bf16[4,3456,128]{2,1,0:T(8,128)(2,1)S(1)} copy-done((bf16[4,3456,128]{2,1,0:T(8,128)(2,1)S(1)}, bf16[4,3456,128]{2,1,0:T(8,128)(2,1)}, u32[]{:S(2)}) %copy-start.2) | copy-done | bytes 3538968
  37.0 0.0 copy-start.3
  37.0 0.9 copy-done.3
  38.0 28.5 %layers.1 = bf16[16,512,128]{2,1,0:T(8,128)(2,1)} custom-call(bf16[8,128,128]{2,1,0:T(8,128)(2,1)S(1)} %copy-done.3, bf16[8,8,128]{2,1,0:T(8,128)(2,1)S(1)} %collective-permute-done.top_ref, bf16[8,8,128]{2,1,0:T(8,128)(2,1)S(1)} %collective-permute-done.1.bottom_ref, bf16[16,768,128]{2,1,0:T(8,128)(2,1)S(1)} %copy-done, ...), custom_call_target="tpu_custom_call" | custom-call | tf_op jit(solution)/shard_map/layers/pallas_call | solution.py:343
  66.6 30.5 %all_to_all.10.in_ref = bf16[16,512,128]{2,1,0:T(8,128)(2,1)S(1)} all-to-all(bf16[16,512,128]{2,1,0:T(8,128)(2,1)} %layers.1), channel_id=1, replica_groups=mesh['bx'=16,'by'=8] {'bx'}, dimensions={0} | all-to-all | bytes 4194304 | tf_op jit(solution)/shard_map/all_to_all | solution.py:430
  97.0 3.7 %transform.1 = bf16[2,64,1,128,128]{4,3,2,1,0:T(8,128)(2,1)} custom-call(bf16[2,512,128]{2,1,0:T(8,128)(2,1)} %constant.2.clone.twiddle_ref, bf16[16,512,128]{2,1,0:T(8,128)(2,1)S(1)} %all_to_all.10.in_ref), custom_call_target="tpu_custom_call" | custom-call | tf_op jit(solution)/shard_map/transform/pallas_call | solution.py:397
Async XLA Ops:
  2.8 22.1 %all-to-all-start = ((f32[128,3,128]{2,1,0:T(4,128)}), f32[128,3,128]{2,1,0:T(4,128)S(1)}, u32[]{:S(2)}, u32[]{:S(2)}) async-start(f32[128,3,128]{2,1,0:T(4,128)} %pack.1), calls=%async_computation | async-start | bytes 524288 | tf_op jit(solution)/shard_map/all_to_all | solution.py:421
  18.8 14.7 %copy-start = (bf16[16,768,128]{2,1,0:T(8,128)(2,1)S(1)}, bf16[16,768,128]{2,1,0:T(8,128)(2,1)}, u32[]{:S(2)}) copy-start(bf16[16,768,128]{2,1,0:T(8,128)(2,1)} %get-tuple-element.10.after_any.r1_ref) | copy-start | bytes 9437188
  28.1 5.5 %collective-permute-start = (bf16[8,8,128]{2,1,0:T(8,128)(2,1)}, bf16[8,8,128]{2,1,0:T(8,128)(2,1)S(1)}, u32[]{:S(2)}, u32[]{:S(2)}) collective-permute-start(bf16[8,8,128]{2,1,0:T(8,128)(2,1)} %get-tuple-element.12), channel_id=1, source_target_pairs={{0,1},{1,2},{2,3},{3,4},{4,5},{5,6},{6,7},{7,0},{8,9},{9,10},{10,1... | collective-permute-start | bytes 49160 | tf_op jit(solution)/shard_map/ppermute | solution.py:426
  28.1 5.5 %collective-permute-start.1 = (bf16[8,8,128]{2,1,0:T(8,128)(2,1)}, bf16[8,8,128]{2,1,0:T(8,128)(2,1)S(1)}, u32[]{:S(2)}, u32[]{:S(2)}) collective-permute-start(bf16[8,8,128]{2,1,0:T(8,128)(2,1)} %get-tuple-element.13), channel_id=1, source_target_pairs={{1,0},{2,1},{3,2},{4,3},{5,4},{6,5},{7,6},{0,7},{9,8},{10,9},{11,1... | collective-permute-start | bytes 49160 | tf_op jit(solution)/shard_map/ppermute | solution.py:427
  33.6 1.5 %copy-start.1 = (bf16[2,3456,128]{2,1,0:T(8,128)(2,1)S(1)}, bf16[2,3456,128]{2,1,0:T(8,128)(2,1)}, u32[]{:S(2)}) copy-start(bf16[2,3456,128]{2,1,0:T(8,128)(2,1)} %late_weights.1.w3_ref) | copy-start | bytes 5308420
  35.0 2.0 %copy-start.2 = (bf16[4,3456,128]{2,1,0:T(8,128)(2,1)S(1)}, bf16[4,3456,128]{2,1,0:T(8,128)(2,1)}, u32[]{:S(2)}) copy-start(bf16[4,3456,128]{2,1,0:T(8,128)(2,1)} %get-tuple-element.14.w2_ref) | copy-start | bytes 10616836
  37.0 0.9 copy-start.3

commit v5 on v4

--- a/solution.py
+++ b/solution.py
@@ -148,7 +148,7 @@
     return pl.pallas_call(
         paint_kernel,
         in_specs=[pl.BlockSpec(memory_space=pltpu.VMEM), pl.BlockSpec(memory_space=pl.ANY)],
-        out_shape=(jax.ShapeDtypeStruct((8, 128, 128), BF16), edge, edge),
+        out_shape=(VMEM((8, 128, 128), BF16), edge, edge),
         scratch_shapes=[VMEM((1024, 256), F32)],
         name="paint",
     )(incoming, after)
@@ -233,15 +233,18 @@
 def late_weights(wout):
     return pl.pallas_call(
         late_weights_kernel,
-        out_shape=jax.ShapeDtypeStruct((2, K_TAPS, 128), BF16),
+        out_shape=VMEM((2, K_TAPS, 128), BF16),
         name="late_weights",
     )(wout)
 
 
 def layers_kernel(
-    painted_ref, top_ref, bottom_ref, r1_ref, w2_ref, w3_ref, out_any,
-    ext_ref, v1_ref, tmp_ref, first_ref, second_ref, rows_ref, third_ref, out_ref, out_sem,
+    painted_ref, top_ref, bottom_ref, r1_ref, w3_ref, w2_any, out_any,
+    w2_ref, ext_ref, v1_ref, tmp_ref, first_ref, second_ref, rows_ref, third_ref, out_ref,
+    in_sem, out_sem,
 ):
+    arrival = pltpu.make_async_copy(w2_any, w2_ref, in_sem)
+    arrival.start()
     ext_ref[:, 144:160] = jnp.zeros((8, 16, 128), F32)
     tmp_ref[:, :, Y1:152] = jnp.zeros((2, 7, 8, 128), F32)
     ext_ref[:, 0:8] = top_ref[...].astype(F32)
@@ -269,6 +272,7 @@
         return carry
 
     lax.fori_loop(0, 8, first_columns, 0)
+    arrival.wait()
 
     low = lax.broadcasted_iota(I32, (5 * Y1, 128), 1) < 64
 
@@ -337,15 +341,16 @@
         copy.wait()
 
 
-def layers(painted, top, bottom, r1, w2, w3):
+def layers(painted, top, bottom, r1, w3, w2):
     whole = pl.BlockSpec(memory_space=pltpu.VMEM)
     anywhere = pl.BlockSpec(memory_space=pl.ANY)
     return pl.pallas_call(
         layers_kernel,
-        in_specs=[whole] * 6,
+        in_specs=[whole] * 5 + [anywhere],
         out_specs=anywhere,
         out_shape=jax.ShapeDtypeStruct((16, 512, 128), BF16),
         scratch_shapes=[
+            VMEM((4, K_TAPS, 128), BF16),
             VMEM((8, 160, 128), F32),
             VMEM((3, 8 * Y1, 128), BF16),
             VMEM((2, 7, 152, 128), F32),
@@ -354,11 +359,12 @@
             VMEM((2, 2, 1024, 128), F32),
             VMEM((4, 512, 128), F32),
             VMEM((16, 512, 128), BF16),
+            pltpu.SemaphoreType.DMA(()),
             pltpu.SemaphoreType.DMA((4,)),
         ],
-        compiler_params=pltpu.CompilerParams(vmem_limit_bytes=44 << 20),
+        compiler_params=pltpu.CompilerParams(vmem_limit_bytes=48 << 20),
         name="layers",
-    )(painted, top, bottom, r1, w2, w3)
+    )(painted, top, bottom, r1, w3, w2)
 
 
 def twiddle_rows(count):
@@ -426,7 +432,7 @@
     top = lax.ppermute(last_y, "by", up_y)
     bottom = lax.ppermute(first_y, "by", down_y)
     w3 = late_weights(weight_out)
-    third = layers(*(in_vmem(v) for v in (painted, top, bottom, r1, w2, w3)))
+    third = layers(*(in_vmem(v) for v in (painted, top, bottom, r1, w3)), w2)
     moved = lax.all_to_all(third, "bx", split_axis=0, concat_axis=0, tiled=True)
     twiddle = jnp.asarray(twiddle_rows(count_x * 8), BF16)
     return transform(twiddle, in_vmem(moved))

time: 101 us -> 98.7 us (0.977)
  local copies, waits for them, and re-layouts: 4.42 us -> 1.89 us
  Pallas kernels: 45.7 us -> 44.4 us
    unnamed x8 -> x2, local copies, waits for them, and re-layouts: 4.42 us -> 1.89 us
    pallas_call x2, Pallas kernels: 31 us -> 29.9 us  [the longest x1 28.6 us: layers(): pl.pallas_call(layers_kernel, in_specs=[whole] * 5 + [anywhere], out_spec...]
  transfers between devices with their start and end apart: 3 -> 3, of which waited for: 1 -> 2; matrix products, arithmetic and copies ran while one was open for 0% -> 0% of each run, Pallas kernels for 7% -> 6%
where the time goes in v5:
time: 98.7 us; the launch traced here: 98.3 us
  Pallas kernels  44.4 us (45%)
  blocking collectives  31.5 us (32%)
  starting transfers between devices  14.1 us (14%)
  waiting for transfers between devices  6.42 us (7%)
  local copies, waits for them, and re-layouts  1.89 us (2%)
    all_to_all x1, blocking collectives, on_device(): moved = lax.all_to_all(third, 'bx', split_axis=0, concat_axis=0, tiled=True)  31.5 us
    pallas_call x1, Pallas kernels, layers(): pl.pallas_call(layers_kernel, in_specs=[whole] * 5 + [anywhere], out_spec...  28.6 us
    all_to_all x1, starting transfers between devices, on_device(): lax.all_to_all(outgoing, ('bx', 'by'), split_axis=0, concat_axis=0, tiled...  11.2 us
    all_to_all x1, waiting for transfers between devices, on_device(): lax.all_to_all(outgoing, ('bx', 'by'), split_axis=0, concat_axis=0, tiled...  6.02 us
    pallas_call x1, Pallas kernels, weights(): pl.pallas_call(weights_kernel, out_shape=(jax.ShapeDtypeStruct((16, 768,...  4.9 us
    pallas_call x1, Pallas kernels, transform(): pl.pallas_call(transform_kernel, grid=(2,), in_specs=[pl.BlockSpec((2, 51...  3.75 us
    pallas_call x1, Pallas kernels, paint(): pl.pallas_call(paint_kernel, in_specs=[pl.BlockSpec(memory_space=pltpu.VM...  3.12 us
    ppermute x1, starting transfers between devices, on_device(): bottom = lax.ppermute(first_y, 'by', down_y)  2.95 us
  transfers between devices with their start and end apart: 3, of which 2 were waited for; matrix products, arithmetic and copies ran while one was open for 0% of the time, Pallas kernels for 6%

profile of v5, /device:TPU:0, one launch (start us, length us, event | category | flops | bytes accessed | tf_op | source)
XLA Modules:
  0.0 98.3 jit_solution(16558952024984340552)
XLA Ops:
  0.0 2.8 %pack.1 = f32[128,3,128]{2,1,0:T(4,128)} custom-call(s32[1,2048]{1,0:T(1,128)} %bitcast.4, s32[1,2048]{1,0:T(1,128)} %bitcast.5, f32[3,2048]{1,0:T(4,128)} %value_ref.1), custom_call_target="tpu_custom_call" | custom-call | tf_op jit(solution)/shard_map/pack/pallas_call | solution.py:75
  2.8 11.2 %all-to-all-start = ((f32[128,3,128]{2,1,0:T(4,128)}), f32[128,3,128]{2,1,0:T(4,128)S(1)}, u32[]{:S(2)}, u32[]{:S(2)}) async-start(f32[128,3,128]{2,1,0:T(4,128)} %pack.1), calls=%async_computation | async-start | bytes 524288 | tf_op jit(solution)/shard_map/all_to_all | solution.py:427
  13.9 4.9 %weights.1 = (bf16[16,768,128]{2,1,0:T(8,128)(2,1)}, bf16[4,3456,128]{2,1,0:T(8,128)(2,1)}) custom-call(bf16[3,9,3,64]{3,2,1,0:T(4,128)(2,1)} %bitcast.3, bf16[3,3,64,192]{3,2,1,0:T(8,128)(2,1)} %wmid_ref.1), custom_call_target="tpu_custom_call" | custom-call | tf_op jit(solution)/shard_map/weights/pallas_call | solution.py:223
  18.8 6.0 %all-to-all-done.in_ref = f32[128,3,128]{2,1,0:T(4,128)S(1)} async-done(((f32[128,3,128]{2,1,0:T(4,128)}), f32[128,3,128]{2,1,0:T(4,128)S(1)}, u32[]{:S(2)}, u32[]{:S(2)}) %all-to-all-start) | async-done | bytes 196640 | tf_op jit(solution)/shard_map/all_to_all | solution.py:427
  24.9 3.1 %paint.1 = (bf16[8,128,128]{2,1,0:T(8,128)(2,1)S(1)}, bf16[8,8,128]{2,1,0:T(8,128)(2,1)}, bf16[8,8,128]{2,1,0:T(8,128)(2,1)}) custom-call(f32[128,3,128]{2,1,0:T(4,128)S(1)} %all-to-all-done.in_ref, bf16[16,768,128]{2,1,0:T(8,128)(2,1)} %get-tuple-element.10.after_any.r1_ref), custom_call_target="tpu_custom_call" | custom-call | tf_op jit(solution)/shard_map/paint/pallas_call | solution.py:148
  28.0 0.0 collective-permute-start
  28.0 3.0 %collective-permute-start.1 = (bf16[8,8,128]{2,1,0:T(8,128)(2,1)}, bf16[8,8,128]{2,1,0:T(8,128)(2,1)S(1)}, u32[]{:S(2)}, u32[]{:S(2)}) collective-permute-start(bf16[8,8,128]{2,1,0:T(8,128)(2,1)} %get-tuple-element.13), channel_id=1, source_target_pairs={{1,0},{2,1},{3,2},{4,3},{5,4},{6,5},{7,6},{0,7},{9,8},{10,9},{11,1... | collective-permute-start | bytes 49160 | tf_op jit(solution)/shard_map/ppermute | solution.py:433
  30.9 1.3 %late_weights.1.w3_ref = bf16[2,3456,128]{2,1,0:T(8,128)(2,1)S(1)} custom-call(bf16[3,3,64,192]{3,2,1,0:T(8,128)(2,1)} %wout_ref.1), custom_call_target="tpu_custom_call" | custom-call | tf_op jit(solution)/shard_map/late_weights/pallas_call | solution.py:234
  32.2 0.4 collective-permute-done.top_ref
  32.6 0.0 collective-permute-done.1.bottom_ref
  32.6 0.0 copy-start
  32.6 1.9 %copy-done = bf16[16,768,128]{2,1,0:T(8,128)(2,1)S(1)} copy-done((bf16[16,768,128]{2,1,0:T(8,128)(2,1)S(1)}, bf16[16,768,128]{2,1,0:T(8,128)(2,1)}, u32[]{:S(2)}) %copy-start) | copy-done | bytes 3145752
  34.5 28.6 %layers.1 = bf16[16,512,128]{2,1,0:T(8,128)(2,1)} custom-call(bf16[8,128,128]{2,1,0:T(8,128)(2,1)S(1)} %get-tuple-element.11.painted_ref, bf16[8,8,128]{2,1,0:T(8,128)(2,1)S(1)} %collective-permute-done.top_ref, bf16[8,8,128]{2,1,0:T(8,128)(2,1)S(1)} %collective-permute-done.1.bottom_ref, bf16[16,768,128]{2,1,0:T(8,128)(2,1)S(1)} %copy-done, ...), custom_call_target="tpu_custom_call" | custom-call | tf_op jit(solution)/shard_map/layers/pallas_call | solution.py:347
  63.1 31.5 %all_to_all.10.in_ref = bf16[16,512,128]{2,1,0:T(8,128)(2,1)S(1)} all-to-all(bf16[16,512,128]{2,1,0:T(8,128)(2,1)} %layers.1), channel_id=1, replica_groups=mesh['bx'=16,'by'=8] {'bx'}, dimensions={0} | all-to-all | bytes 4194304 | tf_op jit(solution)/shard_map/all_to_all | solution.py:436
  94.6 3.7 %transform.1 = bf16[2,64,1,128,128]{4,3,2,1,0:T(8,128)(2,1)} custom-call(bf16[2,512,128]{2,1,0:T(8,128)(2,1)} %constant.2.clone.twiddle_ref, bf16[16,512,128]{2,1,0:T(8,128)(2,1)S(1)} %all_to_all.10.in_ref), custom_call_target="tpu_custom_call" | custom-call | tf_op jit(solution)/shard_map/transform/pallas_call | solution.py:403
Async XLA Ops:
  2.8 22.1 %all-to-all-start = ((f32[128,3,128]{2,1,0:T(4,128)}), f32[128,3,128]{2,1,0:T(4,128)S(1)}, u32[]{:S(2)}, u32[]{:S(2)}) async-start(f32[128,3,128]{2,1,0:T(4,128)} %pack.1), calls=%async_computation | async-start | bytes 524288 | tf_op jit(solution)/shard_map/all_to_all | solution.py:427
  28.0 4.6 %collective-permute-start = (bf16[8,8,128]{2,1,0:T(8,128)(2,1)}, bf16[8,8,128]{2,1,0:T(8,128)(2,1)S(1)}, u32[]{:S(2)}, u32[]{:S(2)}) collective-permute-start(bf16[8,8,128]{2,1,0:T(8,128)(2,1)} %get-tuple-element.12), channel_id=1, source_target_pairs={{0,1},{1,2},{2,3},{3,4},{4,5},{5,6},{6,7},{7,0},{8,9},{9,10},{10,1... | collective-permute-start | bytes 49160 | tf_op jit(solution)/shard_map/ppermute | solution.py:432
  28.0 4.6 %collective-permute-start.1 = (bf16[8,8,128]{2,1,0:T(8,128)(2,1)}, bf16[8,8,128]{2,1,0:T(8,128)(2,1)S(1)}, u32[]{:S(2)}, u32[]{:S(2)}) collective-permute-start(bf16[8,8,128]{2,1,0:T(8,128)(2,1)} %get-tuple-element.13), channel_id=1, source_target_pairs={{1,0},{2,1},{3,2},{4,3},{5,4},{6,5},{7,6},{0,7},{9,8},{10,9},{11,1... | collective-permute-start | bytes 49160 | tf_op jit(solution)/shard_map/ppermute | solution.py:433
  32.6 1.9 %copy-start = (bf16[16,768,128]{2,1,0:T(8,128)(2,1)S(1)}, bf16[16,768,128]{2,1,0:T(8,128)(2,1)}, u32[]{:S(2)}) copy-start(bf16[16,768,128]{2,1,0:T(8,128)(2,1)} %get-tuple-element.10.after_any.r1_ref) | copy-start | bytes 9437188
